TPU v7x, 128 devices: a whole 4x4x4 slice. The times are simulated.
128 devices in a mesh: node: 16 (over y, z), local: 8 (over x, core).
Axes of the slice: x: 4, y: 4, z: 4, core: 2. Of those that a mesh axis runs over, the one named last changes fastest.
Arguments:
- tokens: bfloat16 [8192, 3584], P(('node', 'local')), may hold values from -6 to 6
- expert_ids: int32 [8192, 8], P(('node', 'local')), may hold values from 0 to 63, all different within a row; in each aligned block of 64 rows (0 to 63, 64 to 127, ...) at most 12 rows name the same one
- gate_values: float32 [8192, 8], P(('node', 'local')), may hold values from 0.1 to 1
- holder: int32 [64], replicated, may hold values from 0 to 63, each once
- matching: int32 [16], replicated, may hold values from 0 to 15, as said below
- gate_weight: bfloat16 [128, 3584, 512], P(('node', 'local')), may hold values from -0.09375 to 0.09375
- up_weight: bfloat16 [128, 3584, 512], P(('node', 'local')), may hold values from -0.09375 to 0.09375
- down_weight: bfloat16 [128, 512, 3584], P(('node', 'local')), may hold values from -0.1875 to 0.1875
Outputs:
- moe_out: bfloat16 [8192, 3584], P(('node', 'local'))
- new_gate: bfloat16 [128, 3584, 512], P(('node', 'local'))
- new_up: bfloat16 [128, 3584, 512], P(('node', 'local'))
- new_down: bfloat16 [128, 512, 3584], P(('node', 'local'))
Inputs may be any that keep to these rules, and one draw needn't show every extreme that they name: `expert_ids`: each row names 8 different experts. In the 64 rows of one device no expert is named more than 12 times, and some device names some expert exactly 12 times. `holder`: each expert appears once. A perfect matching of the nodes: matching[matching[n]] == n and matching[n] != n.
All inputs are finite; a program needn't handle non-finite values.
Results may differ from a plain program's by a relative error of at most 0.0065.
Values may be sent and summed in bfloat16 or wider, within the bound.
No kernel may reach another device: no remote copies, remote signals or barrier semaphores. Data moves between devices by JAX's collectives and lax.ppermute only.
A program may use at most 192 MiB of HBM per device.

v0:
```python
import jax
import jax.numpy as jnp
from jax import lax
from jax.sharding import PartitionSpec as P


CAP_NUM, CAP_DEN = 3, 2
BF = jnp.bfloat16
F32 = jnp.float32


HOPS = (0, -1, 1, 2)


def along_x(block, hops, chips):
    pairs = [
        (2 * x + core, 2 * ((x + hops) % chips) + core) for x in range(chips) for core in range(2)
    ]
    return lax.ppermute(block, "local", pairs)


def along_node(block, axis, hops):
    side = 4
    if axis == "y":
        pairs = [(y * side + z, ((y + hops) % side) * side + z) for y in range(side) for z in range(side)]
    else:
        pairs = [(y * side + z, y * side + (z + hops) % side) for y in range(side) for z in range(side)]
    return lax.ppermute(block, "node", pairs)


def from_ring(block, axis):
    return [block] + [along_node(block, axis, -hops) for hops in HOPS[1:]]


def scatter_ring(blocks, axis):
    parts = [blocks[0]] + [along_node(blocks[i], axis, HOPS[i]) for i in (1, 2, 3)]
    return sum(p.astype(F32) for p in parts).astype(BF)


def other_core(block):
    size = lax.axis_size("local")
    return lax.ppermute(block, "local", [(i, i ^ 1) for i in range(size)])


def split_parts(matrix, pieces):
    return matrix.reshape((pieces, matrix.shape[1] // pieces, matrix.shape[2]))


def swap_weight(part, matching):
    nodes = lax.axis_size("node")
    arrived = lax.all_to_all(split_parts(part, nodes), "node", split_axis=0, concat_axis=0, tiled=True)
    reordered = jnp.take(arrived, matching, axis=0, mode="clip")
    returned = lax.all_to_all(reordered, "node", split_axis=0, concat_axis=0, tiled=True)
    return returned.reshape(part.shape)


def half_expert(rows, gate_part, up_part, down_part):
    gate_proj = jnp.dot(rows, gate_part, preferred_element_type=F32)
    up_proj = jnp.dot(rows, up_part, preferred_element_type=F32)
    hidden = (jax.nn.silu(gate_proj) * up_proj).astype(BF)
    return jnp.dot(hidden, down_part, preferred_element_type=F32).astype(BF)


def layer(
    tokens, expert_ids, gate_values, holder, matching, gate_weight, up_weight, down_weight
):
    experts = holder.shape[0]
    tok_count, top_count = expert_ids.shape
    capacity = max(2, tok_count * top_count * CAP_NUM // (CAP_DEN * experts))
    feature_count = tokens.shape[1]
    nodes = lax.axis_size("node")
    chips = lax.axis_size("local") // 2
    my_node = lax.axis_index("node")
    my_chip = lax.axis_index("local") // 2
    weights = (gate_weight, up_weight, down_weight)

    pad = jnp.zeros((tok_count, 128 - 2 * top_count), BF)
    sent = jnp.concatenate(
        [tokens, expert_ids.astype(BF), gate_values.astype(BF), pad], axis=1
    )
    half = tok_count // 2
    first = jnp.concatenate(from_ring(sent[:half], "y"), axis=0)
    second = jnp.concatenate(from_ring(sent[half:], "z"), axis=0)
    first, second = lax.optimization_barrier((first, second))
    pieces = from_ring(first, "z") + from_ring(second, "y")
    total = nodes * tok_count
    gathered = jnp.concatenate(pieces, axis=0)
    token_rows = gathered[:, :feature_count]

    def in_order(columns):
        one = columns[: total // 2].reshape(4, 4, half, -1)
        two = columns[total // 2 :].reshape(4, 4, half, -1).transpose(1, 0, 2, 3)
        return jnp.concatenate([one, two], axis=2).reshape(total, -1)

    def as_rows(columns):
        both = columns.reshape(4, 4, 2, half, -1)
        one = both[:, :, 0].reshape(total // 2, -1)
        two = both[:, :, 1].transpose(1, 0, 2, 3).reshape(total // 2, -1)
        return jnp.concatenate([one, two], axis=0)

    routes = in_order(gathered[:, feature_count : feature_count + 2 * top_count])
    ids = routes[:, :top_count].astype(jnp.int32)
    gates = routes[:, top_count:].astype(F32)

    chip_order = (my_chip + jnp.arange(chips)) % chips
    here = holder[my_node * chips + chip_order]
    match = ids[:, :, None] == here[None, None, :]
    routed = jnp.any(match, axis=1)
    gate_of = jnp.sum(jnp.where(match, gates[:, :, None], 0.0), axis=1)
    before = (jnp.arange(tok_count)[:, None] > jnp.arange(tok_count)[None, :]).astype(BF)
    position = jnp.einsum(
        "ij,sjx->six",
        before,
        routed.astype(BF).reshape(nodes, tok_count, chips),
        preferred_element_type=F32,
    ).reshape(total, chips)
    source = (jnp.arange(total) // tok_count)[:, None]
    key = jnp.where(routed, source * capacity + position.astype(jnp.int32), -1)
    key = as_rows(key)
    gate_of = as_rows(gate_of)
    slots = nodes * capacity
    slot_range = jnp.arange(slots)

    blocks = []
    for hops in range(chips):
        pick = (slot_range[:, None] == key[None, :, hops]).astype(BF)
        blocks.append(jnp.dot(pick, token_rows, preferred_element_type=F32).astype(BF))
    rows = [blocks[0]] + [along_x(blocks[hops], hops, chips) for hops in range(1, chips)]
    rows = jnp.concatenate(rows, axis=0)
    mine = [w[0] for w in weights]
    others = [other_core(w) for w in mine]
    own = half_expert(rows, *mine)
    value = (own.astype(F32) + half_expert(rows, *others).astype(F32)).astype(BF)
    back = [value[:slots]] + [
        along_x(value[hops * slots : (hops + 1) * slots], -hops, chips) for hops in range(1, chips)
    ]
    weighted = [
        jnp.where(key[:, hops, None] == slot_range[None, :], gate_of[:, hops, None], 0.0).astype(BF)
        for hops in range(chips)
    ]
    partial = jnp.dot(
        jnp.concatenate(weighted, axis=1), jnp.concatenate(back, axis=0), preferred_element_type=F32
    ).astype(BF)
    one = partial[: total // 2].reshape(4, 4 * half, feature_count)
    two = partial[total // 2 :].reshape(4, 4 * half, feature_count)
    one = scatter_ring([one[i] for i in range(4)], "z").reshape(4, half, feature_count)
    two = scatter_ring([two[i] for i in range(4)], "y").reshape(4, half, feature_count)
    one, two = lax.optimization_barrier((one, two))
    one = scatter_ring([one[i] for i in range(4)], "y")
    two = scatter_ring([two[i] for i in range(4)], "z")
    combined = jnp.concatenate([one, two], axis=0)
    swapped = [swap_weight(w, matching) for w in weights]
    return (combined, *swapped)


def solution(mesh):
    both = ("node", "local")
    in_specs = (
        P(both, None),
        P(both, None),
        P(both, None),
        P(),
        P(),
        P(both, None, None),
        P(both, None, None),
        P(both, None, None),
    )
    out_specs = (P(both, None), P(both, None, None), P(both, None, None), P(both, None, None))
    return jax.shard_map(layer, mesh=mesh, in_specs=in_specs, out_specs=out_specs, check_vma=False)
```

profile of v0, /device:TPU:82, one launch (start us, length us, event | category | flops | bytes accessed | tf_op | source)
XLA Modules:
  0.0 507.8 jit_solution(16670043591946654580)
XLA Ops:
  3.8 2.4 collective-permute-start.1
  6.2 3.1 collective-permute-start.4
  9.3 4.4 collective-permute-done.2
  13.7 1.6 collective-permute-start.3
  15.3 1.3 collective-permute-done.1
  18.5 1.5 collective-permute-done.3
  20.1 2.6 collective-permute-start.9
  22.7 3.0 collective-permute-start.11
  25.7 1.6 collective-permute-start.6
  27.7 16.4 %collective-permute-done.9 = bf16[128,3712]{1,0:T(8,128)(2,1)S(1)} collective-permute-done((bf16[128,3712]{1,0:T(8,128)(2,1)S(1)}, bf16[128,3712]{1,0:T(8,128)(2,1)S(1)}, u32[]{:S(2)}, u32[]{:S(2)}) %collective-permute-start.9) | collective-permute-done | bytes 950304 | tf_op jit(solution)/shard_map/ppermute | solution.py:28
  45.2 10.0 %all-to-all-start = ((bf16[16,224,512]{2,1,0:T(8,128)(2,1)}), bf16[16,224,512]{2,1,0:T(8,128)(2,1)}, u32[]{:S(2)}, u32[]{:S(2)}) async-start(bf16[16,224,512]{2,1,0:T(8,128)(2,1)} %bitcast.89), calls=%async_computation | async-start | bytes 7340032 | tf_op jit(solution)/shard_map/all_to_all | solution.py:51
  57.0 8.7 %collective-permute-done.11 = bf16[128,3712]{1,0:T(8,128)(2,1)} collective-permute-done((bf16[128,3712]{1,0:T(8,128)(2,1)S(1)}, bf16[128,3712]{1,0:T(8,128)(2,1)}, u32[]{:S(2)}, u32[]{:S(2)}) %collective-permute-start.11) | collective-permute-done | bytes 950304 | tf_op jit(solution)/shard_map/ppermute | solution.py:28
  66.6 10.5 %collective-permute-done.8 = bf16[128,3712]{1,0:T(8,128)(2,1)} collective-permute-done((bf16[128,3712]{1,0:T(8,128)(2,1)S(1)}, bf16[128,3712]{1,0:T(8,128)(2,1)}, u32[]{:S(2)}, u32[]{:S(2)}) %collective-permute-start.8) | collective-permute-done | bytes 950304 | tf_op jit(solution)/shard_map/ppermute | solution.py:28
  78.6 2.2 constant_dynamic-update-slice_fusion.10
  80.8 2.2 constant_dynamic-update-slice_fusion.9
  83.0 2.2 constant_dynamic-update-slice_fusion.8
  87.9 2.2 constant_dynamic-update-slice_fusion.5
  90.1 2.2 constant_dynamic-update-slice_fusion.4
  92.3 5.9 %convolution_convert_fusion.3 = bf16[192,3584]{1,0:T(8,128)(2,1)} fusion(bf16[1024,3712]{1,0:T(8,128)(2,1)} %constant_dynamic-update-slice_fusion.4, s32[1024]{0:T(1024)S(1)} %bitcast.104), kind=kOutput, calls=%fused_computation.16 | convolution fusion | flops 1410170880 | bytes 8720384 | tf_op jit(solution)/shard_map/dot_general | solution.py:127
  98.8 2.7 convolution_convert_fusion.4
  101.4 2.4 collective-permute-start.13
  103.9 2.7 convolution_convert_fusion.5
  106.5 1.8 collective-permute-start.12
  108.3 7.2 %all-to-all-done = bf16[16,224,512]{2,1,0:T(8,128)(2,1)} async-done(((bf16[16,224,512]{2,1,0:T(8,128)(2,1)}), bf16[16,224,512]{2,1,0:T(8,128)(2,1)}, u32[]{:S(2)}, u32[]{:S(2)}) %all-to-all-start) | async-done | bytes 3670048 | tf_op jit(solution)/shard_map/all_to_all | solution.py:51
  115.5 8.9 %all-to-all-start.2 = ((bf16[16,224,512]{2,1,0:T(8,128)(2,1)}), bf16[16,224,512]{2,1,0:T(8,128)(2,1)}, u32[]{:S(2)}, u32[]{:S(2)}) async-start(bf16[16,224,512]{2,1,0:T(8,128)(2,1)} %bitcast.33), calls=%async_computation.2 | async-start | bytes 7340032 | tf_op jit(solution)/shard_map/all_to_all | solution.py:51
  125.8 4.7 convolution_convert_fusion.6
  130.6 19.4 %collective-permute-done.13 = bf16[192,3584]{1,0:T(8,128)(2,1)S(1)} collective-permute-done((bf16[192,3584]{1,0:T(8,128)(2,1)}, bf16[192,3584]{1,0:T(8,128)(2,1)S(1)}, u32[]{:S(2)}, u32[]{:S(2)}) %collective-permute-start.13) | collective-permute-done | bytes 1376288 | tf_op jit(solution)/shard_map/ppermute | solution.py:19
  150.0 3.7 collective-permute-done.12
  153.7 3.6 pad_maximum_fusion
  157.4 7.1 %fusion.40 = f32[768,512]{1,0:T(8,128)S(1)} fusion(bf16[768,3584]{1,0:T(8,128)(2,1)S(1)} %pad_maximum_fusion, bf16[1,3584,512]{2,1,0:T(8,128)(2,1)} %param.14), kind=kOutput, calls=%fused_computation.114 | convolution fusion | flops 2818572288 | bytes 10747904 | tf_op jit(solution)/shard_map/dot_general | solution.py:59
  164.4 4.2 fusion.42
  168.6 9.9 %all-to-all-start.4 = ((bf16[16,32,3584]{2,1,0:T(8,128)(2,1)}), bf16[16,32,3584]{2,1,0:T(8,128)(2,1)}, u32[]{:S(2)}, u32[]{:S(2)}) async-start(bf16[16,32,3584]{2,1,0:T(8,128)(2,1)} %bitcast.92), calls=%async_computation.4 | async-start | bytes 7340032 | tf_op jit(solution)/shard_map/all_to_all | solution.py:51
  178.5 8.1 %convolution_convert_fusion.2 = bf16[768,3584]{1,0:T(8,128)(2,1)} fusion(f32[768,512]{1,0:T(8,128)S(1)} %fusion.40, f32[768,512]{1,0:T(8,128)} %fusion.42, bf16[1,512,3584]{2,1,0:T(8,128)(2,1)} %param.15), kind=kOutput, calls=%fused_computation.7 | convolution fusion | flops 2823684096 | bytes 12320768 | tf_op jit(solution)/shard_map/dot_general | solution.py:61
  186.5 4.7 gather_fusion.1
  191.2 6.1 %fusion.55 = f32[768,512]{1,0:T(8,128)S(1)} fusion(bf16[768,3584]{1,0:T(8,128)(2,1)} %copy-done.2, bf16[3584,512]{1,0:T(8,128)(2,1)} %collective-permute-done.15), kind=kOutput, calls=%fused_computation.128 | convolution fusion | flops 2818572288 | bytes 10747904 | tf_op jit(solution)/shard_map/dot_general | solution.py:58
  197.3 12.5 %add_convert_fusion = bf16[768,3584]{1,0:T(8,128)(2,1)} fusion(bf16[768,3584]{1,0:T(8,128)(2,1)} %convolution_convert_fusion.2, bf16[512,3584]{1,0:T(8,128)(2,1)} %collective-permute-done.17, f32[768,512]{1,0:T(8,128)S(1)} %fusion.55, bf16[768,3584]{1,0:T(8,128)(2,1)} %copy-done.2, bf16[3584,512]{1,0:T(8,128)(2,1)} %collective-permute-done.16), kind=kOutput, calls=%fused_computation.4 | convolution fusion | flops 5653266432 | bytes 25427968 | tf_op jit(solution)/shard_map/dot_general | solution.py:61
  209.8 14.3 %all-to-all-done.4 = bf16[16,32,3584]{2,1,0:T(8,128)(2,1)} async-done(((bf16[16,32,3584]{2,1,0:T(8,128)(2,1)}), bf16[16,32,3584]{2,1,0:T(8,128)(2,1)}, u32[]{:S(2)}, u32[]{:S(2)}) %all-to-all-start.4) | async-done | bytes 3670048 | tf_op jit(solution)/shard_map/all_to_all | solution.py:51
  224.1 10.4 %all-to-all-start.1 = ((bf16[16,224,512]{2,1,0:T(8,128)(2,1)}), bf16[16,224,512]{2,1,0:T(8,128)(2,1)}, u32[]{:S(2)}, u32[]{:S(2)}) async-start(bf16[16,224,512]{2,1,0:T(8,128)(2,1)} %gather_fusion.1), calls=%async_computation.1 | async-start | bytes 7340032 | tf_op jit(solution)/shard_map/all_to_all | solution.py:53
  234.5 4.6 fusion.47
  239.1 6.7 %collective-permute-start.20 = (bf16[192,3584]{1,0:T(8,128)(2,1)}, bf16[192,3584]{1,0:T(8,128)(2,1)}, u32[]{:S(2)}, u32[]{:S(2)}) collective-permute-start(bf16[192,3584]{1,0:T(8,128)(2,1)} %get-tuple-element.21), channel_id=1, source_target_pairs={{0,2},{1,3},{2,4},{3,5},{4,6},{5,7},{6,0},{7,1},{8,10},{9,11},{10,... | collective-permute-start | bytes 4128776 | tf_op jit(solution)/shard_map/ppermute | solution.py:19
  245.8 3.3 collective-permute-start.19
  252.9 4.7 gather_fusion.2
  257.6 20.8 %collective-permute-done.20 = bf16[192,3584]{1,0:T(8,128)(2,1)} collective-permute-done((bf16[192,3584]{1,0:T(8,128)(2,1)}, bf16[192,3584]{1,0:T(8,128)(2,1)}, u32[]{:S(2)}, u32[]{:S(2)}) %collective-permute-start.20) | collective-permute-done | bytes 1376288 | tf_op jit(solution)/shard_map/ppermute | solution.py:19
  278.4 2.3 collective-permute-done.19
  280.7 26.7 %collective-permute-done.18 = bf16[192,3584]{1,0:T(8,128)(2,1)} collective-permute-done((bf16[192,3584]{1,0:T(8,128)(2,1)S(1)}, bf16[192,3584]{1,0:T(8,128)(2,1)}, u32[]{:S(2)}, u32[]{:S(2)}) %collective-permute-start.18) | collective-permute-done | bytes 1376288 | tf_op jit(solution)/shard_map/ppermute | solution.py:19
  307.3 10.7 %convolution_convert_fusion = bf16[1024,3584]{1,0:T(8,128)(2,1)} fusion(bf16[192,3584]{1,0:T(8,128)(2,1)} %collective-permute-done.20, bf16[192,3584]{1,0:T(8,128)(2,1)} %collective-permute-done.19, bf16[192,3584]{1,0:T(8,128)(2,1)} %collective-permute-done.18, bf16[192,3584]{1,0:T(8,128)(2,1)S(1)} %get-tuple-element.20, ...), kind=kOutput, calls=%fused_computation.5 | convolution fusion | flops 5669126144 | bytes 14417920 | tf_op jit(solution)/shard_map/dot_general | solution.py:141
  318.0 7.2 %all-to-all-start.3 = ((bf16[16,224,512]{2,1,0:T(8,128)(2,1)}), bf16[16,224,512]{2,1,0:T(8,128)(2,1)}, u32[]{:S(2)}, u32[]{:S(2)}) async-start(bf16[16,224,512]{2,1,0:T(8,128)(2,1)} %gather_fusion.2), calls=%async_computation.3 | async-start | bytes 7340032 | tf_op jit(solution)/shard_map/all_to_all | solution.py:53
  325.3 4.8 fusion.46
  330.6 2.1 collective-permute-start.25
  333.2 2.1 collective-permute-start.22
  335.3 56.5 %collective-permute-done.26 = bf16[128,3584]{1,0:T(8,128)(2,1)S(1)} collective-permute-done((bf16[128,3584]{1,0:T(8,128)(2,1)S(1)}, bf16[128,3584]{1,0:T(8,128)(2,1)S(1)}, u32[]{:S(2)}, u32[]{:S(2)}) %collective-permute-start.26) | collective-permute-done | bytes 917536 | tf_op jit(solution)/shard_map/ppermute | solution.py:28
  391.8 3.1 collective-permute-start.21
  394.9 4.7 gather_fusion.3
  399.6 8.5 %collective-permute-done.25 = bf16[128,3584]{1,0:T(8,128)(2,1)S(1)} collective-permute-done((bf16[128,3584]{1,0:T(8,128)(2,1)}, bf16[128,3584]{1,0:T(8,128)(2,1)S(1)}, u32[]{:S(2)}, u32[]{:S(2)}) %collective-permute-start.25) | collective-permute-done | bytes 917536 | tf_op jit(solution)/shard_map/ppermute | solution.py:28
  408.0 3.0 collective-permute-done.24
  412.7 3.8 add_convert_fusion.1
  416.5 19.4 %all-to-all-start.5 = ((bf16[16,32,3584]{2,1,0:T(8,128)(2,1)}), bf16[16,32,3584]{2,1,0:T(8,128)(2,1)}, u32[]{:S(2)}, u32[]{:S(2)}) async-start(bf16[16,32,3584]{2,1,0:T(8,128)(2,1)} %gather_fusion.3), calls=%async_computation.5 | async-start | bytes 7340032 | tf_op jit(solution)/shard_map/all_to_all | solution.py:53
  436.6 2.1 collective-permute-start.31
  439.4 2.2 collective-permute-start.28
  441.6 46.5 %collective-permute-done.32 = bf16[32,3584]{1,0:T(8,128)(2,1)S(1)} collective-permute-done((bf16[32,3584]{1,0:T(8,128)(2,1)S(1)}, bf16[32,3584]{1,0:T(8,128)(2,1)S(1)}, u32[]{:S(2)}, u32[]{:S(2)}) %collective-permute-start.32) | collective-permute-done | bytes 229408 | tf_op jit(solution)/shard_map/ppermute | solution.py:28
  488.3 5.9 %collective-permute-done.27 = bf16[32,3584]{1,0:T(8,128)(2,1)S(1)} collective-permute-done((bf16[32,3584]{1,0:T(8,128)(2,1)S(1)}, bf16[32,3584]{1,0:T(8,128)(2,1)S(1)}, u32[]{:S(2)}, u32[]{:S(2)}) %collective-permute-start.27) | collective-permute-done | bytes 229408 | tf_op jit(solution)/shard_map/ppermute | solution.py:28
  495.0 4.1 copy.49
  499.2 4.1 copy.50
  503.3 4.1 copy.51
  (110 shorter events, 24.5 us)
Async XLA Ops:
  0.6 54.6 %copy-start = (s32[64]{0:T(128)S(1)}, s32[64]{0:T(128)}, u32[]{:S(2)}) copy-start(s32[64]{0:T(128)} %param.11) | copy-start | bytes 772
  3.4 10.3 %collective-permute-start.2 = (bf16[32,3712]{1,0:T(8,128)(2,1)S(1)}, bf16[32,3712]{1,0:T(8,128)(2,1)S(1)}, u32[]{:S(2)}, u32[]{:S(2)}) collective-permute-start(bf16[32,3712]{1,0:T(8,128)(2,1)S(1)} %get-tuple-element.31), channel_id=1, source_target_pairs={{0,64},{8,72},{16,80},{24,88},{32,96},{40,104},{48,112},{56,120},{... | collective-permute-start | bytes 712712 | tf_op jit(solution)/shard_map/ppermute | solution.py:28
  3.8 12.8 %collective-permute-start.1 = (bf16[32,3712]{1,0:T(8,128)(2,1)S(1)}, bf16[32,3712]{1,0:T(8,128)(2,1)S(1)}, u32[]{:S(2)}, u32[]{:S(2)}) collective-permute-start(bf16[32,3712]{1,0:T(8,128)(2,1)S(1)} %get-tuple-element.31), channel_id=1, source_target_pairs={{0,96},{8,104},{16,112},{24,120},{32,0},{40,8},{48,16},{56,24},{64... | collective-permute-start | bytes 712712 | tf_op jit(solution)/shard_map/ppermute | solution.py:28
  6.2 11.4 %collective-permute-start = (bf16[32,3712]{1,0:T(8,128)(2,1)S(1)}, bf16[32,3712]{1,0:T(8,128)(2,1)S(1)}, u32[]{:S(2)}, u32[]{:S(2)}) collective-permute-start(bf16[32,3712]{1,0:T(8,128)(2,1)S(1)} %get-tuple-element.31), channel_id=1, source_target_pairs={{0,32},{8,40},{16,48},{24,56},{32,64},{40,72},{48,80},{56,88},{64,... | collective-permute-start | bytes 712712 | tf_op jit(solution)/shard_map/ppermute | solution.py:28
  6.2 11.5 %collective-permute-start.5 = (bf16[32,3712]{1,0:T(8,128)(2,1)S(1)}, bf16[32,3712]{1,0:T(8,128)(2,1)S(1)}, u32[]{:S(2)}, u32[]{:S(2)}) collective-permute-start(bf16[32,3712]{1,0:T(8,128)(2,1)S(1)} %get-tuple-element.30), channel_id=1, source_target_pairs={{0,16},{8,24},{16,0},{24,8},{32,48},{40,56},{48,32},{56,40},{64,80... | collective-permute-start | bytes 712712 | tf_op jit(solution)/shard_map/ppermute | solution.py:28
  6.2 12.2 %collective-permute-start.4 = (bf16[32,3712]{1,0:T(8,128)(2,1)S(1)}, bf16[32,3712]{1,0:T(8,128)(2,1)S(1)}, u32[]{:S(2)}, u32[]{:S(2)}) collective-permute-start(bf16[32,3712]{1,0:T(8,128)(2,1)S(1)} %get-tuple-element.30), channel_id=1, source_target_pairs={{0,24},{8,0},{16,8},{24,16},{32,56},{40,32},{48,40},{56,48},{64,88... | collective-permute-start | bytes 712712 | tf_op jit(solution)/shard_map/ppermute | solution.py:28
  13.7 6.3 %collective-permute-start.3 = (bf16[32,3712]{1,0:T(8,128)(2,1)S(1)}, bf16[32,3712]{1,0:T(8,128)(2,1)S(1)}, u32[]{:S(2)}, u32[]{:S(2)}) collective-permute-start(bf16[32,3712]{1,0:T(8,128)(2,1)S(1)} %get-tuple-element.30), channel_id=1, source_target_pairs={{0,8},{8,16},{16,24},{24,0},{32,40},{40,48},{48,56},{56,32},{64,72... | collective-permute-start | bytes 712712 | tf_op jit(solution)/shard_map/ppermute | solution.py:28
  20.1 24.0 %collective-permute-start.9 = (bf16[128,3712]{1,0:T(8,128)(2,1)S(1)}, bf16[128,3712]{1,0:T(8,128)(2,1)S(1)}, u32[]{:S(2)}, u32[]{:S(2)}) collective-permute-start(bf16[128,3712]{1,0:T(8,128)(2,1)S(1)} %pad_maximum_fusion.2), channel_id=1, source_target_pairs={{0,32},{8,40},{16,48},{24,56},{32,64},{40,72},{48,80},{56,88},{64,... | collective-permute-start | bytes 2850824 | tf_op jit(solution)/shard_map/ppermute | solution.py:28
  22.7 34.3 %collective-permute-start.10 = (bf16[128,3712]{1,0:T(8,128)(2,1)S(1)}, bf16[128,3712]{1,0:T(8,128)(2,1)}, u32[]{:S(2)}, u32[]{:S(2)}) collective-permute-start(bf16[128,3712]{1,0:T(8,128)(2,1)S(1)} %pad_maximum_fusion.2), channel_id=1, source_target_pairs={{0,96},{8,104},{16,112},{24,120},{32,0},{40,8},{48,16},{56,24},{64... | collective-permute-start | bytes 2850824 | tf_op jit(solution)/shard_map/ppermute | solution.py:28
  22.7 42.9 %collective-permute-start.11 = (bf16[128,3712]{1,0:T(8,128)(2,1)S(1)}, bf16[128,3712]{1,0:T(8,128)(2,1)}, u32[]{:S(2)}, u32[]{:S(2)}) collective-permute-start(bf16[128,3712]{1,0:T(8,128)(2,1)S(1)} %pad_maximum_fusion.2), channel_id=1, source_target_pairs={{0,64},{8,72},{16,80},{24,88},{32,96},{40,104},{48,112},{56,120},{... | collective-permute-start | bytes 2850824 | tf_op jit(solution)/shard_map/ppermute | solution.py:28
  25.7 40.8 %collective-permute-start.6 = (bf16[128,3712]{1,0:T(8,128)(2,1)S(1)}, bf16[128,3712]{1,0:T(8,128)(2,1)}, u32[]{:S(2)}, u32[]{:S(2)}) collective-permute-start(bf16[128,3712]{1,0:T(8,128)(2,1)S(1)} %pad_maximum_fusion.1), channel_id=1, source_target_pairs={{0,8},{8,16},{16,24},{24,0},{32,40},{40,48},{48,56},{56,32},{64,72... | collective-permute-start | bytes 2850824 | tf_op jit(solution)/shard_map/ppermute | solution.py:28
  27.3 39.2 %collective-permute-start.7 = (bf16[128,3712]{1,0:T(8,128)(2,1)S(1)}, bf16[128,3712]{1,0:T(8,128)(2,1)}, u32[]{:S(2)}, u32[]{:S(2)}) collective-permute-start(bf16[128,3712]{1,0:T(8,128)(2,1)S(1)} %pad_maximum_fusion.1), channel_id=1, source_target_pairs={{0,24},{8,0},{16,8},{24,16},{32,56},{40,32},{48,40},{56,48},{64,88... | collective-permute-start | bytes 2850824 | tf_op jit(solution)/shard_map/ppermute | solution.py:28
  44.1 32.9 %collective-permute-start.8 = (bf16[128,3712]{1,0:T(8,128)(2,1)S(1)}, bf16[128,3712]{1,0:T(8,128)(2,1)}, u32[]{:S(2)}, u32[]{:S(2)}) collective-permute-start(bf16[128,3712]{1,0:T(8,128)(2,1)S(1)} %pad_maximum_fusion.1), channel_id=1, source_target_pairs={{0,16},{8,24},{16,0},{24,8},{32,48},{40,56},{48,32},{56,40},{64,80... | collective-permute-start | bytes 2850824 | tf_op jit(solution)/shard_map/ppermute | solution.py:28
  45.2 70.3 %all-to-all-start = ((bf16[16,224,512]{2,1,0:T(8,128)(2,1)}), bf16[16,224,512]{2,1,0:T(8,128)(2,1)}, u32[]{:S(2)}, u32[]{:S(2)}) async-start(bf16[16,224,512]{2,1,0:T(8,128)(2,1)} %bitcast.89), calls=%async_computation | async-start | bytes 7340032 | tf_op jit(solution)/shard_map/all_to_all | solution.py:51
  92.3 6.4 %copy-start.6 = (bf16[1024,3712]{1,0:T(8,128)(2,1)S(1)}, bf16[1024,3712]{1,0:T(8,128)(2,1)}, u32[]{:S(2)}) copy-start(bf16[1024,3712]{1,0:T(8,128)(2,1)} %constant_dynamic-update-slice_fusion.4) | copy-start | bytes 22806532
  98.2 32.3 %collective-permute-start.14 = (bf16[192,3584]{1,0:T(8,128)(2,1)}, bf16[192,3584]{1,0:T(8,128)(2,1)S(1)}, u32[]{:S(2)}, u32[]{:S(2)}) collective-permute-start(bf16[192,3584]{1,0:T(8,128)(2,1)} %convolution_convert_fusion.3), channel_id=1, source_target_pairs={{0,6},{1,7},{2,0},{3,1},{4,2},{5,3},{6,4},{7,5},{8,14},{9,15},{10,... | collective-permute-start | bytes 4128776 | tf_op jit(solution)/shard_map/ppermute | solution.py:19
  101.4 48.6 %collective-permute-start.13 = (bf16[192,3584]{1,0:T(8,128)(2,1)}, bf16[192,3584]{1,0:T(8,128)(2,1)S(1)}, u32[]{:S(2)}, u32[]{:S(2)}) collective-permute-start(bf16[192,3584]{1,0:T(8,128)(2,1)} %convolution_convert_fusion.4), channel_id=1, source_target_pairs={{0,4},{1,5},{2,6},{3,7},{4,0},{5,1},{6,2},{7,3},{8,12},{9,13},{10,... | collective-permute-start | bytes 4128776 | tf_op jit(solution)/shard_map/ppermute | solution.py:19
  106.5 47.2 %collective-permute-start.12 = (bf16[192,3584]{1,0:T(8,128)(2,1)}, bf16[192,3584]{1,0:T(8,128)(2,1)}, u32[]{:S(2)}, u32[]{:S(2)}) collective-permute-start(bf16[192,3584]{1,0:T(8,128)(2,1)} %convolution_convert_fusion.5), channel_id=1, source_target_pairs={{0,2},{1,3},{2,4},{3,5},{4,6},{5,7},{6,0},{7,1},{8,10},{9,11},{10,... | collective-permute-start | bytes 4128776 | tf_op jit(solution)/shard_map/ppermute | solution.py:19
  115.5 9.7 %copy-start.7 = (s32[16]{0:T(128)S(1)}, s32[16]{0:T(128)}, u32[]{:S(2)}) copy-start(s32[16]{0:T(128)} %param.12) | copy-start | bytes 196
  115.5 53.1 %all-to-all-start.2 = ((bf16[16,224,512]{2,1,0:T(8,128)(2,1)}), bf16[16,224,512]{2,1,0:T(8,128)(2,1)}, u32[]{:S(2)}, u32[]{:S(2)}) async-start(bf16[16,224,512]{2,1,0:T(8,128)(2,1)} %bitcast.33), calls=%async_computation.2 | async-start | bytes 7340032 | tf_op jit(solution)/shard_map/all_to_all | solution.py:51
  124.5 72.8 %collective-permute-start.17 = (bf16[512,3584]{1,0:T(8,128)(2,1)}, bf16[512,3584]{1,0:T(8,128)(2,1)}, u32[]{:S(2)}, u32[]{:S(2)}) collective-permute-start(bf16[512,3584]{1,0:T(8,128)(2,1)} %bitcast.91), channel_id=1, source_target_pairs={{0,1},{1,0},{2,3},{3,2},{4,5},{5,4},{6,7},{7,6},{8,9},{9,8},{10,11... | collective-permute-start | bytes 11010056 | tf_op jit(solution)/shard_map/ppermute | solution.py:42
  124.7 66.5 %collective-permute-start.15 = (bf16[3584,512]{1,0:T(8,128)(2,1)}, bf16[3584,512]{1,0:T(8,128)(2,1)}, u32[]{:S(2)}, u32[]{:S(2)}) collective-permute-start(bf16[3584,512]{1,0:T(8,128)(2,1)} %bitcast.90), channel_id=1, source_target_pairs={{0,1},{1,0},{2,3},{3,2},{4,5},{5,4},{6,7},{7,6},{8,9},{9,8},{10,11... | collective-permute-start | bytes 11010056 | tf_op jit(solution)/shard_map/ppermute | solution.py:42
  130.6 66.7 %collective-permute-start.16 = (bf16[3584,512]{1,0:T(8,128)(2,1)}, bf16[3584,512]{1,0:T(8,128)(2,1)}, u32[]{:S(2)}, u32[]{:S(2)}) collective-permute-start(bf16[3584,512]{1,0:T(8,128)(2,1)} %bitcast.19), channel_id=1, source_target_pairs={{0,1},{1,0},{2,3},{3,2},{4,5},{5,4},{6,7},{7,6},{8,9},{9,8},{10,11... | collective-permute-start | bytes 11010056 | tf_op jit(solution)/shard_map/ppermute | solution.py:42
  157.3 7.1 %copy-start.2 = (bf16[768,3584]{1,0:T(8,128)(2,1)}, bf16[768,3584]{1,0:T(8,128)(2,1)S(1)}, u32[]{:S(2)}) copy-start(bf16[768,3584]{1,0:T(8,128)(2,1)S(1)} %pad_maximum_fusion) | copy-start | bytes 16515076
  157.3 7.1 %copy-start.3 = (bf16[1,3584,512]{2,1,0:T(8,128)(2,1)S(1)}, bf16[1,3584,512]{2,1,0:T(8,128)(2,1)}, u32[]{:S(2)}) copy-start(bf16[1,3584,512]{2,1,0:T(8,128)(2,1)} %param.13) | copy-start | bytes 11010052
  168.6 55.5 %all-to-all-start.4 = ((bf16[16,32,3584]{2,1,0:T(8,128)(2,1)}), bf16[16,32,3584]{2,1,0:T(8,128)(2,1)}, u32[]{:S(2)}, u32[]{:S(2)}) async-start(bf16[16,32,3584]{2,1,0:T(8,128)(2,1)} %bitcast.92), calls=%async_computation.4 | async-start | bytes 7340032 | tf_op jit(solution)/shard_map/all_to_all | solution.py:51
  224.1 93.9 %all-to-all-start.1 = ((bf16[16,224,512]{2,1,0:T(8,128)(2,1)}), bf16[16,224,512]{2,1,0:T(8,128)(2,1)}, u32[]{:S(2)}, u32[]{:S(2)}) async-start(bf16[16,224,512]{2,1,0:T(8,128)(2,1)} %gather_fusion.1), calls=%async_computation.1 | async-start | bytes 7340032 | tf_op jit(solution)/shard_map/all_to_all | solution.py:53
  239.1 39.3 %collective-permute-start.20 = (bf16[192,3584]{1,0:T(8,128)(2,1)}, bf16[192,3584]{1,0:T(8,128)(2,1)}, u32[]{:S(2)}, u32[]{:S(2)}) collective-permute-start(bf16[192,3584]{1,0:T(8,128)(2,1)} %get-tuple-element.21), channel_id=1, source_target_pairs={{0,2},{1,3},{2,4},{3,5},{4,6},{5,7},{6,0},{7,1},{8,10},{9,11},{10,... | collective-permute-start | bytes 4128776 | tf_op jit(solution)/shard_map/ppermute | solution.py:19
  245.8 34.9 %collective-permute-start.19 = (bf16[192,3584]{1,0:T(8,128)(2,1)}, bf16[192,3584]{1,0:T(8,128)(2,1)}, u32[]{:S(2)}, u32[]{:S(2)}) collective-permute-start(bf16[192,3584]{1,0:T(8,128)(2,1)} %get-tuple-element.22), channel_id=1, source_target_pairs={{0,4},{1,5},{2,6},{3,7},{4,0},{5,1},{6,2},{7,3},{8,12},{9,13},{10,... | collective-permute-start | bytes 4128776 | tf_op jit(solution)/shard_map/ppermute | solution.py:19
  249.1 58.2 %collective-permute-start.18 = (bf16[192,3584]{1,0:T(8,128)(2,1)S(1)}, bf16[192,3584]{1,0:T(8,128)(2,1)}, u32[]{:S(2)}, u32[]{:S(2)}) collective-permute-start(bf16[192,3584]{1,0:T(8,128)(2,1)S(1)} %get-tuple-element.23), channel_id=1, source_target_pairs={{0,6},{1,7},{2,0},{3,1},{4,2},{5,3},{6,4},{7,5},{8,14},{9,15},{10,... | collective-permute-start | bytes 4128776 | tf_op jit(solution)/shard_map/ppermute | solution.py:19
  318.0 98.5 %all-to-all-start.3 = ((bf16[16,224,512]{2,1,0:T(8,128)(2,1)}), bf16[16,224,512]{2,1,0:T(8,128)(2,1)}, u32[]{:S(2)}, u32[]{:S(2)}) async-start(bf16[16,224,512]{2,1,0:T(8,128)(2,1)} %gather_fusion.2), calls=%async_computation.3 | async-start | bytes 7340032 | tf_op jit(solution)/shard_map/all_to_all | solution.py:53
  330.0 61.8 %collective-permute-start.26 = (bf16[128,3584]{1,0:T(8,128)(2,1)S(1)}, bf16[128,3584]{1,0:T(8,128)(2,1)S(1)}, u32[]{:S(2)}, u32[]{:S(2)}) collective-permute-start(bf16[128,3584]{1,0:T(8,128)(2,1)S(1)} %get-tuple-element.15), channel_id=1, source_target_pairs={{0,64},{8,72},{16,80},{24,88},{32,96},{40,104},{48,112},{56,120},{... | collective-permute-start | bytes 2752520 | tf_op jit(solution)/shard_map/ppermute | solution.py:28
  330.6 77.5 %collective-permute-start.25 = (bf16[128,3584]{1,0:T(8,128)(2,1)}, bf16[128,3584]{1,0:T(8,128)(2,1)S(1)}, u32[]{:S(2)}, u32[]{:S(2)}) collective-permute-start(bf16[128,3584]{1,0:T(8,128)(2,1)} %get-tuple-element.16), channel_id=1, source_target_pairs={{0,32},{8,40},{16,48},{24,56},{32,64},{40,72},{48,80},{56,88},{64,... | collective-permute-start | bytes 2752520 | tf_op jit(solution)/shard_map/ppermute | solution.py:28
  332.6 78.4 %collective-permute-start.24 = (bf16[128,3584]{1,0:T(8,128)(2,1)}, bf16[128,3584]{1,0:T(8,128)(2,1)S(1)}, u32[]{:S(2)}, u32[]{:S(2)}) collective-permute-start(bf16[128,3584]{1,0:T(8,128)(2,1)} %get-tuple-element.14), channel_id=1, source_target_pairs={{0,96},{8,104},{16,112},{24,120},{32,0},{40,8},{48,16},{56,24},{64... | collective-permute-start | bytes 2752520 | tf_op jit(solution)/shard_map/ppermute | solution.py:28
  332.7 78.4 %collective-permute-start.23 = (bf16[128,3584]{1,0:T(8,128)(2,1)}, bf16[128,3584]{1,0:T(8,128)(2,1)}, u32[]{:S(2)}, u32[]{:S(2)}) collective-permute-start(bf16[128,3584]{1,0:T(8,128)(2,1)} %get-tuple-element.17), channel_id=1, source_target_pairs={{0,16},{8,24},{16,0},{24,8},{32,48},{40,56},{48,32},{56,40},{64,80... | collective-permute-start | bytes 2752520 | tf_op jit(solution)/shard_map/ppermute | solution.py:28
  333.2 77.8 %collective-permute-start.22 = (bf16[128,3584]{1,0:T(8,128)(2,1)}, bf16[128,3584]{1,0:T(8,128)(2,1)}, u32[]{:S(2)}, u32[]{:S(2)}) collective-permute-start(bf16[128,3584]{1,0:T(8,128)(2,1)} %get-tuple-element.18), channel_id=1, source_target_pairs={{0,8},{8,16},{16,24},{24,0},{32,40},{40,48},{48,56},{56,32},{64,72... | collective-permute-start | bytes 2752520 | tf_op jit(solution)/shard_map/ppermute | solution.py:28
  391.8 20.8 %collective-permute-start.21 = (bf16[128,3584]{1,0:T(8,128)(2,1)}, bf16[128,3584]{1,0:T(8,128)(2,1)}, u32[]{:S(2)}, u32[]{:S(2)}) collective-permute-start(bf16[128,3584]{1,0:T(8,128)(2,1)} %get-tuple-element.19), channel_id=1, source_target_pairs={{0,24},{8,0},{16,8},{24,16},{32,56},{40,32},{48,40},{56,48},{64,88... | collective-permute-start | bytes 2752520 | tf_op jit(solution)/shard_map/ppermute | solution.py:28
  408.0 3.0 copy-start.4
  411.0 0.9 copy-start.5
  416.5 78.5 %all-to-all-start.5 = ((bf16[16,32,3584]{2,1,0:T(8,128)(2,1)}), bf16[16,32,3584]{2,1,0:T(8,128)(2,1)}, u32[]{:S(2)}, u32[]{:S(2)}) async-start(bf16[16,32,3584]{2,1,0:T(8,128)(2,1)} %gather_fusion.3), calls=%async_computation.5 | async-start | bytes 7340032 | tf_op jit(solution)/shard_map/all_to_all | solution.py:53
  436.0 52.1 %collective-permute-start.32 = (bf16[32,3584]{1,0:T(8,128)(2,1)S(1)}, bf16[32,3584]{1,0:T(8,128)(2,1)S(1)}, u32[]{:S(2)}, u32[]{:S(2)}) collective-permute-start(bf16[32,3584]{1,0:T(8,128)(2,1)S(1)} %get-tuple-element.28), channel_id=1, source_target_pairs={{0,16},{8,24},{16,0},{24,8},{32,48},{40,56},{48,32},{56,40},{64,80... | collective-permute-start | bytes 688136 | tf_op jit(solution)/shard_map/ppermute | solution.py:28
  436.6 51.5 %collective-permute-start.31 = (bf16[32,3584]{1,0:T(8,128)(2,1)S(1)}, bf16[32,3584]{1,0:T(8,128)(2,1)S(1)}, u32[]{:S(2)}, u32[]{:S(2)}) collective-permute-start(bf16[32,3584]{1,0:T(8,128)(2,1)S(1)} %get-tuple-element.29), channel_id=1, source_target_pairs={{0,8},{8,16},{16,24},{24,0},{32,40},{40,48},{48,56},{56,32},{64,72... | collective-permute-start | bytes 688136 | tf_op jit(solution)/shard_map/ppermute | solution.py:28
  438.7 49.4 %collective-permute-start.30 = (bf16[32,3584]{1,0:T(8,128)(2,1)S(1)}, bf16[32,3584]{1,0:T(8,128)(2,1)S(1)}, u32[]{:S(2)}, u32[]{:S(2)}) collective-permute-start(bf16[32,3584]{1,0:T(8,128)(2,1)S(1)} %get-tuple-element.27), channel_id=1, source_target_pairs={{0,24},{8,0},{16,8},{24,16},{32,56},{40,32},{48,40},{56,48},{64,88... | collective-permute-start | bytes 688136 | tf_op jit(solution)/shard_map/ppermute | solution.py:28
  438.7 49.5 %collective-permute-start.29 = (bf16[32,3584]{1,0:T(8,128)(2,1)S(1)}, bf16[32,3584]{1,0:T(8,128)(2,1)S(1)}, u32[]{:S(2)}, u32[]{:S(2)}) collective-permute-start(bf16[32,3584]{1,0:T(8,128)(2,1)S(1)} %get-tuple-element.25), channel_id=1, source_target_pairs={{0,64},{8,72},{16,80},{24,88},{32,96},{40,104},{48,112},{56,120},{... | collective-permute-start | bytes 688136 | tf_op jit(solution)/shard_map/ppermute | solution.py:28
  439.4 48.9 %collective-permute-start.28 = (bf16[32,3584]{1,0:T(8,128)(2,1)S(1)}, bf16[32,3584]{1,0:T(8,128)(2,1)S(1)}, u32[]{:S(2)}, u32[]{:S(2)}) collective-permute-start(bf16[32,3584]{1,0:T(8,128)(2,1)S(1)} %get-tuple-element.26), channel_id=1, source_target_pairs={{0,32},{8,40},{16,48},{24,56},{32,64},{40,72},{48,80},{56,88},{64,... | collective-permute-start | bytes 688136 | tf_op jit(solution)/shard_map/ppermute | solution.py:28
  488.1 6.0 %collective-permute-start.27 = (bf16[32,3584]{1,0:T(8,128)(2,1)S(1)}, bf16[32,3584]{1,0:T(8,128)(2,1)S(1)}, u32[]{:S(2)}, u32[]{:S(2)}) collective-permute-start(bf16[32,3584]{1,0:T(8,128)(2,1)S(1)} %get-tuple-element.24), channel_id=1, source_target_pairs={{0,96},{8,104},{16,112},{24,120},{32,0},{40,8},{48,16},{56,24},{64... | collective-permute-start | bytes 688136 | tf_op jit(solution)/shard_map/ppermute | solution.py:28
  499.2 8.2 %copy-start.1 = (s32[64]{0:T(128)S(1)}, s32[64]{0:T(128)}, u32[]{:S(2)}) copy-start(s32[64]{0:T(128)} %param.11) | copy-start | bytes 772
where the time goes:
time: 517 us; the launch traced here: 508 us
  waiting for transfers between devices  260 us (50%)
  starting transfers between devices  112 us (22%)
  matrix products  64.6 us (12%)
  local copies, waits for them, and re-layouts  54.3 us (11%)
  other arithmetic  15.9 us (3%)
    ppermute x24, waiting for transfers between devices, along_node(): return lax.ppermute(block, 'node', pairs)  166 us
    ppermute x6, waiting for transfers between devices, along_x(): return lax.ppermute(block, 'local', pairs)  72.9 us
    all_to_all x3, starting transfers between devices, swap_weight(): lax.all_to_all(reordered, 'node', split_axis=0, concat_axis=0, tiled=True)  37 us
    ppermute x24, starting transfers between devices, along_node(): return lax.ppermute(block, 'node', pairs)  30.2 us
    all_to_all x3, starting transfers between devices, swap_weight(): lax.all_to_all(split_parts(part, nodes), 'node', split_axis=0, concat_axi...  28.8 us
    unnamed x28, local copies, waits for them, and re-layouts  25.2 us
    all_to_all x3, waiting for transfers between devices, swap_weight(): lax.all_to_all(split_parts(part, nodes), 'node', split_axis=0, concat_axi...  21.4 us
    dot_general x2, matrix products, half_expert(): return jnp.dot(hidden, down_part, preferred_element_type=F32).astype(BF)  20.6 us
  transfers between devices with their start and end apart: 39, of which 22 were waited for; matrix products, arithmetic and copies ran while one was open for 23% of the time, Pallas kernels for 0%

commit v1 on v0

--- a/solution.py
+++ b/solution.py
@@ -1,6 +1,7 @@
 import jax
 import jax.numpy as jnp
 from jax import lax
+from jax.experimental import pallas as pl
 from jax.sharding import PartitionSpec as P
 
 
@@ -46,12 +47,31 @@
     return matrix.reshape((pieces, matrix.shape[1] // pieces, matrix.shape[2]))
 
 
-def swap_weight(part, matching):
+def swap_weight(part, matching, name):
     nodes = lax.axis_size("node")
     arrived = lax.all_to_all(split_parts(part, nodes), "node", split_axis=0, concat_axis=0, tiled=True)
     reordered = jnp.take(arrived, matching, axis=0, mode="clip")
     returned = lax.all_to_all(reordered, "node", split_axis=0, concat_axis=0, tiled=True)
-    return returned.reshape(part.shape)
+    if name == "d":
+        return returned.reshape(part.shape)
+    return keep(returned.reshape(part.shape[1:]), 4).reshape(part.shape)
+
+
+def copy_kernel(in_ref, out_ref):
+    out_ref[...] = in_ref[...]
+
+
+def keep(matrix, steps):
+    rows, columns = matrix.shape
+    spec = pl.BlockSpec((rows // steps, columns), lambda i: (i, 0))
+    return pl.pallas_call(
+        copy_kernel,
+        out_shape=jax.ShapeDtypeStruct(matrix.shape, matrix.dtype),
+        grid=(steps,),
+        in_specs=[spec],
+        out_specs=spec,
+        cost_estimate=pl.CostEstimate(flops=0, bytes_accessed=4 * rows * columns, transcendentals=0),
+    )(matrix)
 
 
 def half_expert(rows, gate_part, up_part, down_part):
@@ -149,7 +169,7 @@
     one = scatter_ring([one[i] for i in range(4)], "y")
     two = scatter_ring([two[i] for i in range(4)], "z")
     combined = jnp.concatenate([one, two], axis=0)
-    swapped = [swap_weight(w, matching) for w in weights]
+    swapped = [swap_weight(w, matching, name) for w, name in zip(weights, "gud")]
     return (combined, *swapped)
 
 

time: 517 us -> 518 us (level)
  Pallas kernels: 0 us -> 8.85 us
  local copies, waits for them, and re-layouts: 54.3 us -> 46.1 us
    pallas_call x0 -> x2, Pallas kernels: none -> 8.85 us  [keep(): pl.pallas_call(copy_kernel, out_shape=jax.ShapeDtypeStruct(matrix.shape,...]
    unnamed x28 -> x26, local copies, waits for them, and re-layouts: 25.2 us -> 17 us
  transfers between devices with their start and end apart: 39 -> 39, of which waited for: 22 -> 22; matrix products, arithmetic and copies ran while one was open for 23% -> 23% of each run, Pallas kernels for 0% -> 2%
where the time goes in v1:
time: 518 us; the launch traced here: 508 us
  waiting for transfers between devices  260 us (50%)
  starting transfers between devices  112 us (22%)
  matrix products  64.6 us (12%)
  local copies, waits for them, and re-layouts  46.1 us (9%)
  other arithmetic  15.9 us (3%)
  Pallas kernels  8.85 us (2%)
    ppermute x24, waiting for transfers between devices, along_node(): return lax.ppermute(block, 'node', pairs)  166 us
    ppermute x6, waiting for transfers between devices, along_x(): return lax.ppermute(block, 'local', pairs)  72.9 us
    all_to_all x3, starting transfers between devices, swap_weight(): lax.all_to_all(reordered, 'node', split_axis=0, concat_axis=0, tiled=True)  37 us
    ppermute x24, starting transfers between devices, along_node(): return lax.ppermute(block, 'node', pairs)  30.2 us
    all_to_all x3, starting transfers between devices, swap_weight(): lax.all_to_all(split_parts(part, nodes), 'node', split_axis=0, concat_axi...  28.8 us
    all_to_all x3, waiting for transfers between devices, swap_weight(): lax.all_to_all(split_parts(part, nodes), 'node', split_axis=0, concat_axi...  21.4 us
    dot_general x2, matrix products, half_expert(): return jnp.dot(hidden, down_part, preferred_element_type=F32).astype(BF)  20.6 us
    unnamed x26, local copies, waits for them, and re-layouts  17 us
  transfers between devices with their start and end apart: 39, of which 22 were waited for; matrix products, arithmetic and copies ran while one was open for 23% of the time, Pallas kernels for 2%

profile of v1, /device:TPU:82, one launch (start us, length us, event | category | flops | bytes accessed | tf_op | source)
XLA Modules:
  0.0 508.4 jit_solution(9110573796433857037)
XLA Ops:
  3.8 2.4 collective-permute-start.1
  6.2 3.1 collective-permute-start.4
  9.3 4.4 collective-permute-done.2
  13.7 1.6 collective-permute-start.3
  15.3 1.3 collective-permute-done.1
  18.5 1.5 collective-permute-done.3
  20.1 2.6 collective-permute-start.9
  22.7 3.0 collective-permute-start.11
  25.7 1.6 collective-permute-start.6
  27.7 16.4 %collective-permute-done.9 = bf16[128,3712]{1,0:T(8,128)(2,1)S(1)} collective-permute-done((bf16[128,3712]{1,0:T(8,128)(2,1)S(1)}, bf16[128,3712]{1,0:T(8,128)(2,1)S(1)}, u32[]{:S(2)}, u32[]{:S(2)}) %collective-permute-start.9) | collective-permute-done | bytes 950304 | tf_op jit(solution)/shard_map/ppermute | solution.py:29
  45.2 10.0 %all-to-all-start = ((bf16[16,224,512]{2,1,0:T(8,128)(2,1)}), bf16[16,224,512]{2,1,0:T(8,128)(2,1)}, u32[]{:S(2)}, u32[]{:S(2)}) async-start(bf16[16,224,512]{2,1,0:T(8,128)(2,1)} %bitcast.91), calls=%async_computation | async-start | bytes 7340032 | tf_op jit(solution)/shard_map/all_to_all | solution.py:52
  57.0 8.7 %collective-permute-done.11 = bf16[128,3712]{1,0:T(8,128)(2,1)} collective-permute-done((bf16[128,3712]{1,0:T(8,128)(2,1)S(1)}, bf16[128,3712]{1,0:T(8,128)(2,1)}, u32[]{:S(2)}, u32[]{:S(2)}) %collective-permute-start.11) | collective-permute-done | bytes 950304 | tf_op jit(solution)/shard_map/ppermute | solution.py:29
  66.6 10.5 %collective-permute-done.8 = bf16[128,3712]{1,0:T(8,128)(2,1)} collective-permute-done((bf16[128,3712]{1,0:T(8,128)(2,1)S(1)}, bf16[128,3712]{1,0:T(8,128)(2,1)}, u32[]{:S(2)}, u32[]{:S(2)}) %collective-permute-start.8) | collective-permute-done | bytes 950304 | tf_op jit(solution)/shard_map/ppermute | solution.py:29
  78.6 2.2 constant_dynamic-update-slice_fusion.10
  80.8 2.2 constant_dynamic-update-slice_fusion.9
  83.0 2.2 constant_dynamic-update-slice_fusion.8
  87.9 2.2 constant_dynamic-update-slice_fusion.5
  90.1 2.2 constant_dynamic-update-slice_fusion.4
  92.3 5.9 %convolution_convert_fusion.3 = bf16[192,3584]{1,0:T(8,128)(2,1)} fusion(bf16[1024,3712]{1,0:T(8,128)(2,1)} %constant_dynamic-update-slice_fusion.4, s32[1024]{0:T(1024)S(1)} %bitcast.108), kind=kOutput, calls=%fused_computation.16 | convolution fusion | flops 1410170880 | bytes 8720384 | tf_op jit(solution)/shard_map/dot_general | solution.py:147
  98.8 2.7 convolution_convert_fusion.4
  101.4 2.4 collective-permute-start.13
  103.9 2.7 convolution_convert_fusion.5
  106.5 1.8 collective-permute-start.12
  108.3 7.2 %all-to-all-done = bf16[16,224,512]{2,1,0:T(8,128)(2,1)} async-done(((bf16[16,224,512]{2,1,0:T(8,128)(2,1)}), bf16[16,224,512]{2,1,0:T(8,128)(2,1)}, u32[]{:S(2)}, u32[]{:S(2)}) %all-to-all-start) | async-done | bytes 3670048 | tf_op jit(solution)/shard_map/all_to_all | solution.py:52
  115.5 8.9 %all-to-all-start.2 = ((bf16[16,224,512]{2,1,0:T(8,128)(2,1)}), bf16[16,224,512]{2,1,0:T(8,128)(2,1)}, u32[]{:S(2)}, u32[]{:S(2)}) async-start(bf16[16,224,512]{2,1,0:T(8,128)(2,1)} %bitcast.34), calls=%async_computation.2 | async-start | bytes 7340032 | tf_op jit(solution)/shard_map/all_to_all | solution.py:52
  125.8 4.7 convolution_convert_fusion.6
  130.6 19.4 %collective-permute-done.13 = bf16[192,3584]{1,0:T(8,128)(2,1)S(1)} collective-permute-done((bf16[192,3584]{1,0:T(8,128)(2,1)}, bf16[192,3584]{1,0:T(8,128)(2,1)S(1)}, u32[]{:S(2)}, u32[]{:S(2)}) %collective-permute-start.13) | collective-permute-done | bytes 1376288 | tf_op jit(solution)/shard_map/ppermute | solution.py:20
  150.0 3.7 collective-permute-done.12
  153.7 3.6 pad_maximum_fusion
  157.4 7.1 %fusion.40 = f32[768,512]{1,0:T(8,128)S(1)} fusion(bf16[768,3584]{1,0:T(8,128)(2,1)S(1)} %pad_maximum_fusion, bf16[1,3584,512]{2,1,0:T(8,128)(2,1)} %param.14), kind=kOutput, calls=%fused_computation.114 | convolution fusion | flops 2818572288 | bytes 10747904 | tf_op jit(solution)/shard_map/dot_general | solution.py:79
  164.4 4.2 fusion.42
  168.6 9.9 %all-to-all-start.4 = ((bf16[16,32,3584]{2,1,0:T(8,128)(2,1)}), bf16[16,32,3584]{2,1,0:T(8,128)(2,1)}, u32[]{:S(2)}, u32[]{:S(2)}) async-start(bf16[16,32,3584]{2,1,0:T(8,128)(2,1)} %bitcast.94), calls=%async_computation.4 | async-start | bytes 7340032 | tf_op jit(solution)/shard_map/all_to_all | solution.py:52
  178.5 8.1 %convolution_convert_fusion.2 = bf16[768,3584]{1,0:T(8,128)(2,1)} fusion(f32[768,512]{1,0:T(8,128)S(1)} %fusion.40, f32[768,512]{1,0:T(8,128)} %fusion.42, bf16[1,512,3584]{2,1,0:T(8,128)(2,1)} %param.15), kind=kOutput, calls=%fused_computation.7 | convolution fusion | flops 2823684096 | bytes 12320768 | tf_op jit(solution)/shard_map/dot_general | solution.py:81
  186.5 4.7 gather_fusion.1
  191.2 6.1 %fusion.55 = f32[768,512]{1,0:T(8,128)S(1)} fusion(bf16[768,3584]{1,0:T(8,128)(2,1)} %copy-done.2, bf16[3584,512]{1,0:T(8,128)(2,1)} %collective-permute-done.15), kind=kOutput, calls=%fused_computation.128 | convolution fusion | flops 2818572288 | bytes 10747904 | tf_op jit(solution)/shard_map/dot_general | solution.py:78
  197.3 12.5 %add_convert_fusion = bf16[768,3584]{1,0:T(8,128)(2,1)} fusion(bf16[768,3584]{1,0:T(8,128)(2,1)} %convolution_convert_fusion.2, bf16[512,3584]{1,0:T(8,128)(2,1)} %collective-permute-done.17, f32[768,512]{1,0:T(8,128)S(1)} %fusion.55, bf16[768,3584]{1,0:T(8,128)(2,1)} %copy-done.2, bf16[3584,512]{1,0:T(8,128)(2,1)} %collective-permute-done.16), kind=kOutput, calls=%fused_computation.4 | convolution fusion | flops 5653266432 | bytes 25427968 | tf_op jit(solution)/shard_map/dot_general | solution.py:81
  209.8 14.3 %all-to-all-done.4 = bf16[16,32,3584]{2,1,0:T(8,128)(2,1)} async-done(((bf16[16,32,3584]{2,1,0:T(8,128)(2,1)}), bf16[16,32,3584]{2,1,0:T(8,128)(2,1)}, u32[]{:S(2)}, u32[]{:S(2)}) %all-to-all-start.4) | async-done | bytes 3670048 | tf_op jit(solution)/shard_map/all_to_all | solution.py:52
  224.1 10.4 %all-to-all-start.1 = ((bf16[16,224,512]{2,1,0:T(8,128)(2,1)}), bf16[16,224,512]{2,1,0:T(8,128)(2,1)}, u32[]{:S(2)}, u32[]{:S(2)}) async-start(bf16[16,224,512]{2,1,0:T(8,128)(2,1)} %gather_fusion.1), calls=%async_computation.1 | async-start | bytes 7340032 | tf_op jit(solution)/shard_map/all_to_all | solution.py:54
  234.5 4.6 fusion.47
  239.1 6.7 %collective-permute-start.20 = (bf16[192,3584]{1,0:T(8,128)(2,1)}, bf16[192,3584]{1,0:T(8,128)(2,1)}, u32[]{:S(2)}, u32[]{:S(2)}) collective-permute-start(bf16[192,3584]{1,0:T(8,128)(2,1)} %get-tuple-element.21), channel_id=1, source_target_pairs={{0,2},{1,3},{2,4},{3,5},{4,6},{5,7},{6,0},{7,1},{8,10},{9,11},{10,... | collective-permute-start | bytes 4128776 | tf_op jit(solution)/shard_map/ppermute | solution.py:20
  245.8 3.3 collective-permute-start.19
  252.9 4.7 gather_fusion.2
  257.6 20.8 %collective-permute-done.20 = bf16[192,3584]{1,0:T(8,128)(2,1)} collective-permute-done((bf16[192,3584]{1,0:T(8,128)(2,1)}, bf16[192,3584]{1,0:T(8,128)(2,1)}, u32[]{:S(2)}, u32[]{:S(2)}) %collective-permute-start.20) | collective-permute-done | bytes 1376288 | tf_op jit(solution)/shard_map/ppermute | solution.py:20
  278.4 2.3 collective-permute-done.19
  280.7 26.7 %collective-permute-done.18 = bf16[192,3584]{1,0:T(8,128)(2,1)} collective-permute-done((bf16[192,3584]{1,0:T(8,128)(2,1)S(1)}, bf16[192,3584]{1,0:T(8,128)(2,1)}, u32[]{:S(2)}, u32[]{:S(2)}) %collective-permute-start.18) | collective-permute-done | bytes 1376288 | tf_op jit(solution)/shard_map/ppermute | solution.py:20
  307.3 10.7 %convolution_convert_fusion = bf16[1024,3584]{1,0:T(8,128)(2,1)} fusion(bf16[192,3584]{1,0:T(8,128)(2,1)} %collective-permute-done.20, bf16[192,3584]{1,0:T(8,128)(2,1)} %collective-permute-done.19, bf16[192,3584]{1,0:T(8,128)(2,1)} %collective-permute-done.18, bf16[192,3584]{1,0:T(8,128)(2,1)S(1)} %get-tuple-element.20, ...), kind=kOutput, calls=%fused_computation.5 | convolution fusion | flops 5669126144 | bytes 14417920 | tf_op jit(solution)/shard_map/dot_general | solution.py:161
  318.0 7.2 %all-to-all-start.3 = ((bf16[16,224,512]{2,1,0:T(8,128)(2,1)}), bf16[16,224,512]{2,1,0:T(8,128)(2,1)}, u32[]{:S(2)}, u32[]{:S(2)}) async-start(bf16[16,224,512]{2,1,0:T(8,128)(2,1)} %gather_fusion.2), calls=%async_computation.3 | async-start | bytes 7340032 | tf_op jit(solution)/shard_map/all_to_all | solution.py:54
  325.3 4.8 fusion.46
  330.6 2.1 collective-permute-start.25
  333.2 2.1 collective-permute-start.22
  335.3 56.5 %collective-permute-done.26 = bf16[128,3584]{1,0:T(8,128)(2,1)S(1)} collective-permute-done((bf16[128,3584]{1,0:T(8,128)(2,1)S(1)}, bf16[128,3584]{1,0:T(8,128)(2,1)S(1)}, u32[]{:S(2)}, u32[]{:S(2)}) %collective-permute-start.26) | collective-permute-done | bytes 917536 | tf_op jit(solution)/shard_map/ppermute | solution.py:29
  391.8 3.1 collective-permute-start.21
  394.9 4.7 gather_fusion.3
  399.6 8.5 %collective-permute-done.25 = bf16[128,3584]{1,0:T(8,128)(2,1)S(1)} collective-permute-done((bf16[128,3584]{1,0:T(8,128)(2,1)}, bf16[128,3584]{1,0:T(8,128)(2,1)S(1)}, u32[]{:S(2)}, u32[]{:S(2)}) %collective-permute-start.25) | collective-permute-done | bytes 917536 | tf_op jit(solution)/shard_map/ppermute | solution.py:29
  408.0 3.0 collective-permute-done.24
  412.7 3.8 add_convert_fusion.1
  416.5 19.4 %all-to-all-start.5 = ((bf16[16,32,3584]{2,1,0:T(8,128)(2,1)}), bf16[16,32,3584]{2,1,0:T(8,128)(2,1)}, u32[]{:S(2)}, u32[]{:S(2)}) async-start(bf16[16,32,3584]{2,1,0:T(8,128)(2,1)} %gather_fusion.3), calls=%async_computation.5 | async-start | bytes 7340032 | tf_op jit(solution)/shard_map/all_to_all | solution.py:54
  436.6 2.1 collective-permute-start.31
  439.4 2.2 collective-permute-start.28
  441.6 46.5 %collective-permute-done.32 = bf16[32,3584]{1,0:T(8,128)(2,1)S(1)} collective-permute-done((bf16[32,3584]{1,0:T(8,128)(2,1)S(1)}, bf16[32,3584]{1,0:T(8,128)(2,1)S(1)}, u32[]{:S(2)}, u32[]{:S(2)}) %collective-permute-start.32) | collective-permute-done | bytes 229408 | tf_op jit(solution)/shard_map/ppermute | solution.py:29
  488.3 5.9 %collective-permute-done.27 = bf16[32,3584]{1,0:T(8,128)(2,1)S(1)} collective-permute-done((bf16[32,3584]{1,0:T(8,128)(2,1)S(1)}, bf16[32,3584]{1,0:T(8,128)(2,1)S(1)}, u32[]{:S(2)}, u32[]{:S(2)}) %collective-permute-start.27) | collective-permute-done | bytes 229408 | tf_op jit(solution)/shard_map/ppermute | solution.py:29
  495.0 4.4 shard_map.111
  499.5 4.4 shard_map.112
  503.9 4.1 copy.47
  (110 shorter events, 24.5 us)
Async XLA Ops:
  0.6 54.6 %copy-start = (s32[64]{0:T(128)S(1)}, s32[64]{0:T(128)}, u32[]{:S(2)}) copy-start(s32[64]{0:T(128)} %param.11) | copy-start | bytes 772
  3.4 10.3 %collective-permute-start.2 = (bf16[32,3712]{1,0:T(8,128)(2,1)S(1)}, bf16[32,3712]{1,0:T(8,128)(2,1)S(1)}, u32[]{:S(2)}, u32[]{:S(2)}) collective-permute-start(bf16[32,3712]{1,0:T(8,128)(2,1)S(1)} %get-tuple-element.31), channel_id=1, source_target_pairs={{0,64},{8,72},{16,80},{24,88},{32,96},{40,104},{48,112},{56,120},{... | collective-permute-start | bytes 712712 | tf_op jit(solution)/shard_map/ppermute | solution.py:29
  3.8 12.8 %collective-permute-start.1 = (bf16[32,3712]{1,0:T(8,128)(2,1)S(1)}, bf16[32,3712]{1,0:T(8,128)(2,1)S(1)}, u32[]{:S(2)}, u32[]{:S(2)}) collective-permute-start(bf16[32,3712]{1,0:T(8,128)(2,1)S(1)} %get-tuple-element.31), channel_id=1, source_target_pairs={{0,96},{8,104},{16,112},{24,120},{32,0},{40,8},{48,16},{56,24},{64... | collective-permute-start | bytes 712712 | tf_op jit(solution)/shard_map/ppermute | solution.py:29
  6.2 11.4 %collective-permute-start = (bf16[32,3712]{1,0:T(8,128)(2,1)S(1)}, bf16[32,3712]{1,0:T(8,128)(2,1)S(1)}, u32[]{:S(2)}, u32[]{:S(2)}) collective-permute-start(bf16[32,3712]{1,0:T(8,128)(2,1)S(1)} %get-tuple-element.31), channel_id=1, source_target_pairs={{0,32},{8,40},{16,48},{24,56},{32,64},{40,72},{48,80},{56,88},{64,... | collective-permute-start | bytes 712712 | tf_op jit(solution)/shard_map/ppermute | solution.py:29
  6.2 11.5 %collective-permute-start.5 = (bf16[32,3712]{1,0:T(8,128)(2,1)S(1)}, bf16[32,3712]{1,0:T(8,128)(2,1)S(1)}, u32[]{:S(2)}, u32[]{:S(2)}) collective-permute-start(bf16[32,3712]{1,0:T(8,128)(2,1)S(1)} %get-tuple-element.30), channel_id=1, source_target_pairs={{0,16},{8,24},{16,0},{24,8},{32,48},{40,56},{48,32},{56,40},{64,80... | collective-permute-start | bytes 712712 | tf_op jit(solution)/shard_map/ppermute | solution.py:29
  6.2 12.2 %collective-permute-start.4 = (bf16[32,3712]{1,0:T(8,128)(2,1)S(1)}, bf16[32,3712]{1,0:T(8,128)(2,1)S(1)}, u32[]{:S(2)}, u32[]{:S(2)}) collective-permute-start(bf16[32,3712]{1,0:T(8,128)(2,1)S(1)} %get-tuple-element.30), channel_id=1, source_target_pairs={{0,24},{8,0},{16,8},{24,16},{32,56},{40,32},{48,40},{56,48},{64,88... | collective-permute-start | bytes 712712 | tf_op jit(solution)/shard_map/ppermute | solution.py:29
  13.7 6.3 %collective-permute-start.3 = (bf16[32,3712]{1,0:T(8,128)(2,1)S(1)}, bf16[32,3712]{1,0:T(8,128)(2,1)S(1)}, u32[]{:S(2)}, u32[]{:S(2)}) collective-permute-start(bf16[32,3712]{1,0:T(8,128)(2,1)S(1)} %get-tuple-element.30), channel_id=1, source_target_pairs={{0,8},{8,16},{16,24},{24,0},{32,40},{40,48},{48,56},{56,32},{64,72... | collective-permute-start | bytes 712712 | tf_op jit(solution)/shard_map/ppermute | solution.py:29
  20.1 24.0 %collective-permute-start.9 = (bf16[128,3712]{1,0:T(8,128)(2,1)S(1)}, bf16[128,3712]{1,0:T(8,128)(2,1)S(1)}, u32[]{:S(2)}, u32[]{:S(2)}) collective-permute-start(bf16[128,3712]{1,0:T(8,128)(2,1)S(1)} %pad_maximum_fusion.2), channel_id=1, source_target_pairs={{0,32},{8,40},{16,48},{24,56},{32,64},{40,72},{48,80},{56,88},{64,... | collective-permute-start | bytes 2850824 | tf_op jit(solution)/shard_map/ppermute | solution.py:29
  22.7 34.3 %collective-permute-start.10 = (bf16[128,3712]{1,0:T(8,128)(2,1)S(1)}, bf16[128,3712]{1,0:T(8,128)(2,1)}, u32[]{:S(2)}, u32[]{:S(2)}) collective-permute-start(bf16[128,3712]{1,0:T(8,128)(2,1)S(1)} %pad_maximum_fusion.2), channel_id=1, source_target_pairs={{0,96},{8,104},{16,112},{24,120},{32,0},{40,8},{48,16},{56,24},{64... | collective-permute-start | bytes 2850824 | tf_op jit(solution)/shard_map/ppermute | solution.py:29
  22.7 42.9 %collective-permute-start.11 = (bf16[128,3712]{1,0:T(8,128)(2,1)S(1)}, bf16[128,3712]{1,0:T(8,128)(2,1)}, u32[]{:S(2)}, u32[]{:S(2)}) collective-permute-start(bf16[128,3712]{1,0:T(8,128)(2,1)S(1)} %pad_maximum_fusion.2), channel_id=1, source_target_pairs={{0,64},{8,72},{16,80},{24,88},{32,96},{40,104},{48,112},{56,120},{... | collective-permute-start | bytes 2850824 | tf_op jit(solution)/shard_map/ppermute | solution.py:29
  25.7 40.8 %collective-permute-start.6 = (bf16[128,3712]{1,0:T(8,128)(2,1)S(1)}, bf16[128,3712]{1,0:T(8,128)(2,1)}, u32[]{:S(2)}, u32[]{:S(2)}) collective-permute-start(bf16[128,3712]{1,0:T(8,128)(2,1)S(1)} %pad_maximum_fusion.1), channel_id=1, source_target_pairs={{0,8},{8,16},{16,24},{24,0},{32,40},{40,48},{48,56},{56,32},{64,72... | collective-permute-start | bytes 2850824 | tf_op jit(solution)/shard_map/ppermute | solution.py:29
  27.3 39.2 %collective-permute-start.7 = (bf16[128,3712]{1,0:T(8,128)(2,1)S(1)}, bf16[128,3712]{1,0:T(8,128)(2,1)}, u32[]{:S(2)}, u32[]{:S(2)}) collective-permute-start(bf16[128,3712]{1,0:T(8,128)(2,1)S(1)} %pad_maximum_fusion.1), channel_id=1, source_target_pairs={{0,24},{8,0},{16,8},{24,16},{32,56},{40,32},{48,40},{56,48},{64,88... | collective-permute-start | bytes 2850824 | tf_op jit(solution)/shard_map/ppermute | solution.py:29
  44.1 32.9 %collective-permute-start.8 = (bf16[128,3712]{1,0:T(8,128)(2,1)S(1)}, bf16[128,3712]{1,0:T(8,128)(2,1)}, u32[]{:S(2)}, u32[]{:S(2)}) collective-permute-start(bf16[128,3712]{1,0:T(8,128)(2,1)S(1)} %pad_maximum_fusion.1), channel_id=1, source_target_pairs={{0,16},{8,24},{16,0},{24,8},{32,48},{40,56},{48,32},{56,40},{64,80... | collective-permute-start | bytes 2850824 | tf_op jit(solution)/shard_map/ppermute | solution.py:29
  45.2 70.3 %all-to-all-start = ((bf16[16,224,512]{2,1,0:T(8,128)(2,1)}), bf16[16,224,512]{2,1,0:T(8,128)(2,1)}, u32[]{:S(2)}, u32[]{:S(2)}) async-start(bf16[16,224,512]{2,1,0:T(8,128)(2,1)} %bitcast.91), calls=%async_computation | async-start | bytes 7340032 | tf_op jit(solution)/shard_map/all_to_all | solution.py:52
  92.3 6.4 %copy-start.6 = (bf16[1024,3712]{1,0:T(8,128)(2,1)S(1)}, bf16[1024,3712]{1,0:T(8,128)(2,1)}, u32[]{:S(2)}) copy-start(bf16[1024,3712]{1,0:T(8,128)(2,1)} %constant_dynamic-update-slice_fusion.4) | copy-start | bytes 22806532
  98.2 32.3 %collective-permute-start.14 = (bf16[192,3584]{1,0:T(8,128)(2,1)}, bf16[192,3584]{1,0:T(8,128)(2,1)S(1)}, u32[]{:S(2)}, u32[]{:S(2)}) collective-permute-start(bf16[192,3584]{1,0:T(8,128)(2,1)} %convolution_convert_fusion.3), channel_id=1, source_target_pairs={{0,6},{1,7},{2,0},{3,1},{4,2},{5,3},{6,4},{7,5},{8,14},{9,15},{10,... | collective-permute-start | bytes 4128776 | tf_op jit(solution)/shard_map/ppermute | solution.py:20
  101.4 48.6 %collective-permute-start.13 = (bf16[192,3584]{1,0:T(8,128)(2,1)}, bf16[192,3584]{1,0:T(8,128)(2,1)S(1)}, u32[]{:S(2)}, u32[]{:S(2)}) collective-permute-start(bf16[192,3584]{1,0:T(8,128)(2,1)} %convolution_convert_fusion.4), channel_id=1, source_target_pairs={{0,4},{1,5},{2,6},{3,7},{4,0},{5,1},{6,2},{7,3},{8,12},{9,13},{10,... | collective-permute-start | bytes 4128776 | tf_op jit(solution)/shard_map/ppermute | solution.py:20
  106.5 47.2 %collective-permute-start.12 = (bf16[192,3584]{1,0:T(8,128)(2,1)}, bf16[192,3584]{1,0:T(8,128)(2,1)}, u32[]{:S(2)}, u32[]{:S(2)}) collective-permute-start(bf16[192,3584]{1,0:T(8,128)(2,1)} %convolution_convert_fusion.5), channel_id=1, source_target_pairs={{0,2},{1,3},{2,4},{3,5},{4,6},{5,7},{6,0},{7,1},{8,10},{9,11},{10,... | collective-permute-start | bytes 4128776 | tf_op jit(solution)/shard_map/ppermute | solution.py:20
  115.5 9.7 %copy-start.7 = (s32[16]{0:T(128)S(1)}, s32[16]{0:T(128)}, u32[]{:S(2)}) copy-start(s32[16]{0:T(128)} %param.12) | copy-start | bytes 196
  115.5 53.1 %all-to-all-start.2 = ((bf16[16,224,512]{2,1,0:T(8,128)(2,1)}), bf16[16,224,512]{2,1,0:T(8,128)(2,1)}, u32[]{:S(2)}, u32[]{:S(2)}) async-start(bf16[16,224,512]{2,1,0:T(8,128)(2,1)} %bitcast.34), calls=%async_computation.2 | async-start | bytes 7340032 | tf_op jit(solution)/shard_map/all_to_all | solution.py:52
  124.5 72.8 %collective-permute-start.17 = (bf16[512,3584]{1,0:T(8,128)(2,1)}, bf16[512,3584]{1,0:T(8,128)(2,1)}, u32[]{:S(2)}, u32[]{:S(2)}) collective-permute-start(bf16[512,3584]{1,0:T(8,128)(2,1)} %bitcast.93), channel_id=1, source_target_pairs={{0,1},{1,0},{2,3},{3,2},{4,5},{5,4},{6,7},{7,6},{8,9},{9,8},{10,11... | collective-permute-start | bytes 11010056 | tf_op jit(solution)/shard_map/ppermute | solution.py:43
  124.7 66.5 %collective-permute-start.15 = (bf16[3584,512]{1,0:T(8,128)(2,1)}, bf16[3584,512]{1,0:T(8,128)(2,1)}, u32[]{:S(2)}, u32[]{:S(2)}) collective-permute-start(bf16[3584,512]{1,0:T(8,128)(2,1)} %bitcast.92), channel_id=1, source_target_pairs={{0,1},{1,0},{2,3},{3,2},{4,5},{5,4},{6,7},{7,6},{8,9},{9,8},{10,11... | collective-permute-start | bytes 11010056 | tf_op jit(solution)/shard_map/ppermute | solution.py:43
  130.6 66.7 %collective-permute-start.16 = (bf16[3584,512]{1,0:T(8,128)(2,1)}, bf16[3584,512]{1,0:T(8,128)(2,1)}, u32[]{:S(2)}, u32[]{:S(2)}) collective-permute-start(bf16[3584,512]{1,0:T(8,128)(2,1)} %bitcast.19), channel_id=1, source_target_pairs={{0,1},{1,0},{2,3},{3,2},{4,5},{5,4},{6,7},{7,6},{8,9},{9,8},{10,11... | collective-permute-start | bytes 11010056 | tf_op jit(solution)/shard_map/ppermute | solution.py:43
  157.3 7.1 %copy-start.2 = (bf16[768,3584]{1,0:T(8,128)(2,1)}, bf16[768,3584]{1,0:T(8,128)(2,1)S(1)}, u32[]{:S(2)}) copy-start(bf16[768,3584]{1,0:T(8,128)(2,1)S(1)} %pad_maximum_fusion) | copy-start | bytes 16515076
  157.3 7.1 %copy-start.3 = (bf16[1,3584,512]{2,1,0:T(8,128)(2,1)S(1)}, bf16[1,3584,512]{2,1,0:T(8,128)(2,1)}, u32[]{:S(2)}) copy-start(bf16[1,3584,512]{2,1,0:T(8,128)(2,1)} %param.13) | copy-start | bytes 11010052
  168.6 55.5 %all-to-all-start.4 = ((bf16[16,32,3584]{2,1,0:T(8,128)(2,1)}), bf16[16,32,3584]{2,1,0:T(8,128)(2,1)}, u32[]{:S(2)}, u32[]{:S(2)}) async-start(bf16[16,32,3584]{2,1,0:T(8,128)(2,1)} %bitcast.94), calls=%async_computation.4 | async-start | bytes 7340032 | tf_op jit(solution)/shard_map/all_to_all | solution.py:52
  224.1 93.9 %all-to-all-start.1 = ((bf16[16,224,512]{2,1,0:T(8,128)(2,1)}), bf16[16,224,512]{2,1,0:T(8,128)(2,1)}, u32[]{:S(2)}, u32[]{:S(2)}) async-start(bf16[16,224,512]{2,1,0:T(8,128)(2,1)} %gather_fusion.1), calls=%async_computation.1 | async-start | bytes 7340032 | tf_op jit(solution)/shard_map/all_to_all | solution.py:54
  239.1 39.3 %collective-permute-start.20 = (bf16[192,3584]{1,0:T(8,128)(2,1)}, bf16[192,3584]{1,0:T(8,128)(2,1)}, u32[]{:S(2)}, u32[]{:S(2)}) collective-permute-start(bf16[192,3584]{1,0:T(8,128)(2,1)} %get-tuple-element.21), channel_id=1, source_target_pairs={{0,2},{1,3},{2,4},{3,5},{4,6},{5,7},{6,0},{7,1},{8,10},{9,11},{10,... | collective-permute-start | bytes 4128776 | tf_op jit(solution)/shard_map/ppermute | solution.py:20
  245.8 34.9 %collective-permute-start.19 = (bf16[192,3584]{1,0:T(8,128)(2,1)}, bf16[192,3584]{1,0:T(8,128)(2,1)}, u32[]{:S(2)}, u32[]{:S(2)}) collective-permute-start(bf16[192,3584]{1,0:T(8,128)(2,1)} %get-tuple-element.22), channel_id=1, source_target_pairs={{0,4},{1,5},{2,6},{3,7},{4,0},{5,1},{6,2},{7,3},{8,12},{9,13},{10,... | collective-permute-start | bytes 4128776 | tf_op jit(solution)/shard_map/ppermute | solution.py:20
  249.1 58.2 %collective-permute-start.18 = (bf16[192,3584]{1,0:T(8,128)(2,1)S(1)}, bf16[192,3584]{1,0:T(8,128)(2,1)}, u32[]{:S(2)}, u32[]{:S(2)}) collective-permute-start(bf16[192,3584]{1,0:T(8,128)(2,1)S(1)} %get-tuple-element.23), channel_id=1, source_target_pairs={{0,6},{1,7},{2,0},{3,1},{4,2},{5,3},{6,4},{7,5},{8,14},{9,15},{10,... | collective-permute-start | bytes 4128776 | tf_op jit(solution)/shard_map/ppermute | solution.py:20
  318.0 98.5 %all-to-all-start.3 = ((bf16[16,224,512]{2,1,0:T(8,128)(2,1)}), bf16[16,224,512]{2,1,0:T(8,128)(2,1)}, u32[]{:S(2)}, u32[]{:S(2)}) async-start(bf16[16,224,512]{2,1,0:T(8,128)(2,1)} %gather_fusion.2), calls=%async_computation.3 | async-start | bytes 7340032 | tf_op jit(solution)/shard_map/all_to_all | solution.py:54
  330.0 61.8 %collective-permute-start.26 = (bf16[128,3584]{1,0:T(8,128)(2,1)S(1)}, bf16[128,3584]{1,0:T(8,128)(2,1)S(1)}, u32[]{:S(2)}, u32[]{:S(2)}) collective-permute-start(bf16[128,3584]{1,0:T(8,128)(2,1)S(1)} %get-tuple-element.15), channel_id=1, source_target_pairs={{0,64},{8,72},{16,80},{24,88},{32,96},{40,104},{48,112},{56,120},{... | collective-permute-start | bytes 2752520 | tf_op jit(solution)/shard_map/ppermute | solution.py:29
  330.6 77.5 %collective-permute-start.25 = (bf16[128,3584]{1,0:T(8,128)(2,1)}, bf16[128,3584]{1,0:T(8,128)(2,1)S(1)}, u32[]{:S(2)}, u32[]{:S(2)}) collective-permute-start(bf16[128,3584]{1,0:T(8,128)(2,1)} %get-tuple-element.16), channel_id=1, source_target_pairs={{0,32},{8,40},{16,48},{24,56},{32,64},{40,72},{48,80},{56,88},{64,... | collective-permute-start | bytes 2752520 | tf_op jit(solution)/shard_map/ppermute | solution.py:29
  332.6 78.4 %collective-permute-start.24 = (bf16[128,3584]{1,0:T(8,128)(2,1)}, bf16[128,3584]{1,0:T(8,128)(2,1)S(1)}, u32[]{:S(2)}, u32[]{:S(2)}) collective-permute-start(bf16[128,3584]{1,0:T(8,128)(2,1)} %get-tuple-element.14), channel_id=1, source_target_pairs={{0,96},{8,104},{16,112},{24,120},{32,0},{40,8},{48,16},{56,24},{64... | collective-permute-start | bytes 2752520 | tf_op jit(solution)/shard_map/ppermute | solution.py:29
  332.7 78.4 %collective-permute-start.23 = (bf16[128,3584]{1,0:T(8,128)(2,1)}, bf16[128,3584]{1,0:T(8,128)(2,1)}, u32[]{:S(2)}, u32[]{:S(2)}) collective-permute-start(bf16[128,3584]{1,0:T(8,128)(2,1)} %get-tuple-element.17), channel_id=1, source_target_pairs={{0,16},{8,24},{16,0},{24,8},{32,48},{40,56},{48,32},{56,40},{64,80... | collective-permute-start | bytes 2752520 | tf_op jit(solution)/shard_map/ppermute | solution.py:29
  333.2 77.8 %collective-permute-start.22 = (bf16[128,3584]{1,0:T(8,128)(2,1)}, bf16[128,3584]{1,0:T(8,128)(2,1)}, u32[]{:S(2)}, u32[]{:S(2)}) collective-permute-start(bf16[128,3584]{1,0:T(8,128)(2,1)} %get-tuple-element.18), channel_id=1, source_target_pairs={{0,8},{8,16},{16,24},{24,0},{32,40},{40,48},{48,56},{56,32},{64,72... | collective-permute-start | bytes 2752520 | tf_op jit(solution)/shard_map/ppermute | solution.py:29
  391.8 20.8 %collective-permute-start.21 = (bf16[128,3584]{1,0:T(8,128)(2,1)}, bf16[128,3584]{1,0:T(8,128)(2,1)}, u32[]{:S(2)}, u32[]{:S(2)}) collective-permute-start(bf16[128,3584]{1,0:T(8,128)(2,1)} %get-tuple-element.19), channel_id=1, source_target_pairs={{0,24},{8,0},{16,8},{24,16},{32,56},{40,32},{48,40},{56,48},{64,88... | collective-permute-start | bytes 2752520 | tf_op jit(solution)/shard_map/ppermute | solution.py:29
  408.0 3.0 copy-start.4
  411.0 0.9 copy-start.5
  416.5 87.4 %all-to-all-start.5 = ((bf16[16,32,3584]{2,1,0:T(8,128)(2,1)}), bf16[16,32,3584]{2,1,0:T(8,128)(2,1)}, u32[]{:S(2)}, u32[]{:S(2)}) async-start(bf16[16,32,3584]{2,1,0:T(8,128)(2,1)} %gather_fusion.3), calls=%async_computation.5 | async-start | bytes 7340032 | tf_op jit(solution)/shard_map/all_to_all | solution.py:54
  436.0 52.1 %collective-permute-start.32 = (bf16[32,3584]{1,0:T(8,128)(2,1)S(1)}, bf16[32,3584]{1,0:T(8,128)(2,1)S(1)}, u32[]{:S(2)}, u32[]{:S(2)}) collective-permute-start(bf16[32,3584]{1,0:T(8,128)(2,1)S(1)} %get-tuple-element.28), channel_id=1, source_target_pairs={{0,16},{8,24},{16,0},{24,8},{32,48},{40,56},{48,32},{56,40},{64,80... | collective-permute-start | bytes 688136 | tf_op jit(solution)/shard_map/ppermute | solution.py:29
  436.6 51.5 %collective-permute-start.31 = (bf16[32,3584]{1,0:T(8,128)(2,1)S(1)}, bf16[32,3584]{1,0:T(8,128)(2,1)S(1)}, u32[]{:S(2)}, u32[]{:S(2)}) collective-permute-start(bf16[32,3584]{1,0:T(8,128)(2,1)S(1)} %get-tuple-element.29), channel_id=1, source_target_pairs={{0,8},{8,16},{16,24},{24,0},{32,40},{40,48},{48,56},{56,32},{64,72... | collective-permute-start | bytes 688136 | tf_op jit(solution)/shard_map/ppermute | solution.py:29
  438.7 49.4 %collective-permute-start.30 = (bf16[32,3584]{1,0:T(8,128)(2,1)S(1)}, bf16[32,3584]{1,0:T(8,128)(2,1)S(1)}, u32[]{:S(2)}, u32[]{:S(2)}) collective-permute-start(bf16[32,3584]{1,0:T(8,128)(2,1)S(1)} %get-tuple-element.27), channel_id=1, source_target_pairs={{0,24},{8,0},{16,8},{24,16},{32,56},{40,32},{48,40},{56,48},{64,88... | collective-permute-start | bytes 688136 | tf_op jit(solution)/shard_map/ppermute | solution.py:29
  438.7 49.5 %collective-permute-start.29 = (bf16[32,3584]{1,0:T(8,128)(2,1)S(1)}, bf16[32,3584]{1,0:T(8,128)(2,1)S(1)}, u32[]{:S(2)}, u32[]{:S(2)}) collective-permute-start(bf16[32,3584]{1,0:T(8,128)(2,1)S(1)} %get-tuple-element.25), channel_id=1, source_target_pairs={{0,64},{8,72},{16,80},{24,88},{32,96},{40,104},{48,112},{56,120},{... | collective-permute-start | bytes 688136 | tf_op jit(solution)/shard_map/ppermute | solution.py:29
  439.4 48.9 %collective-permute-start.28 = (bf16[32,3584]{1,0:T(8,128)(2,1)S(1)}, bf16[32,3584]{1,0:T(8,128)(2,1)S(1)}, u32[]{:S(2)}, u32[]{:S(2)}) collective-permute-start(bf16[32,3584]{1,0:T(8,128)(2,1)S(1)} %get-tuple-element.26), channel_id=1, source_target_pairs={{0,32},{8,40},{16,48},{24,56},{32,64},{40,72},{48,80},{56,88},{64,... | collective-permute-start | bytes 688136 | tf_op jit(solution)/shard_map/ppermute | solution.py:29
  488.1 6.0 %collective-permute-start.27 = (bf16[32,3584]{1,0:T(8,128)(2,1)S(1)}, bf16[32,3584]{1,0:T(8,128)(2,1)S(1)}, u32[]{:S(2)}, u32[]{:S(2)}) collective-permute-start(bf16[32,3584]{1,0:T(8,128)(2,1)S(1)} %get-tuple-element.24), channel_id=1, source_target_pairs={{0,96},{8,104},{16,112},{24,120},{32,0},{40,8},{48,16},{56,24},{64... | collective-permute-start | bytes 688136 | tf_op jit(solution)/shard_map/ppermute | solution.py:29
  503.9 4.1 copy-start.1

commit v2 on v1

--- a/solution.py
+++ b/solution.py
@@ -2,6 +2,7 @@
 import jax.numpy as jnp
 from jax import lax
 from jax.experimental import pallas as pl
+from jax.experimental.pallas import tpu as pltpu
 from jax.sharding import PartitionSpec as P
 
 
@@ -33,6 +34,13 @@
     return [block] + [along_node(block, axis, -hops) for hops in HOPS[1:]]
 
 
+def relayed(below, above, axis):
+    half = below.shape[0] // 2
+    return jnp.concatenate(
+        [along_node(below[:half], axis, 1), along_node(above[half:], axis, -1)], axis=0
+    )
+
+
 def scatter_ring(blocks, axis):
     parts = [blocks[0]] + [along_node(blocks[i], axis, HOPS[i]) for i in (1, 2, 3)]
     return sum(p.astype(F32) for p in parts).astype(BF)
@@ -47,13 +55,11 @@
     return matrix.reshape((pieces, matrix.shape[1] // pieces, matrix.shape[2]))
 
 
-def swap_weight(part, matching, name):
+def swap_weight(part, matching):
     nodes = lax.axis_size("node")
     arrived = lax.all_to_all(split_parts(part, nodes), "node", split_axis=0, concat_axis=0, tiled=True)
     reordered = jnp.take(arrived, matching, axis=0, mode="clip")
     returned = lax.all_to_all(reordered, "node", split_axis=0, concat_axis=0, tiled=True)
-    if name == "d":
-        return returned.reshape(part.shape)
     return keep(returned.reshape(part.shape[1:]), 4).reshape(part.shape)
 
 
@@ -72,6 +78,79 @@
         out_specs=spec,
         cost_estimate=pl.CostEstimate(flops=0, bytes_accessed=4 * rows * columns, transcendentals=0),
     )(matrix)
+
+
+def pick_kernel(key_ref, *refs):
+    hops, total = key_ref.shape
+    pieces, outs, pick = refs[: -hops - 1], refs[-hops - 1 : -1], refs[-1]
+    slots = outs[0].shape[0]
+
+    @pl.when(pl.program_id(0) == 0)
+    def _():
+        slot = lax.broadcasted_iota(jnp.int32, (slots, total), 0)
+        for h in range(hops):
+            pick[h * slots : (h + 1) * slots, :] = jnp.where(slot == key_ref[h : h + 1, :], 1.0, 0.0).astype(BF)
+
+    rows = jnp.concatenate([p[...] for p in pieces], axis=0)
+    picked = jnp.dot(pick[...], rows, preferred_element_type=F32)
+    for h in range(hops):
+        outs[h][...] = picked[h * slots : (h + 1) * slots].astype(BF)
+
+
+def pick_rows(key, pieces, slots, columns, tile=512):
+    hops, total = key.shape
+    return pl.pallas_call(
+        pick_kernel,
+        out_shape=[jax.ShapeDtypeStruct((slots, columns), BF)] * hops,
+        grid=(columns // tile,),
+        in_specs=[pl.BlockSpec((hops, total), lambda i: (0, 0))]
+        + [pl.BlockSpec((p.shape[0], tile), lambda i: (0, i)) for p in pieces],
+        out_specs=[pl.BlockSpec((slots, tile), lambda i: (0, i))] * hops,
+        scratch_shapes=[pltpu.VMEM((hops * slots, total), BF)],
+        cost_estimate=pl.CostEstimate(
+            flops=2 * hops * slots * total * columns,
+            bytes_accessed=2 * columns * (total + hops * slots),
+            transcendentals=0,
+        ),
+    )(key, *pieces)
+
+
+def add_kernel(key_ref, gate_ref, *refs):
+    total, hops = key_ref.shape
+    blocks, outs, weigh = refs[:hops], refs[hops:-1], refs[-1]
+    slots = blocks[0].shape[0]
+
+    @pl.when(pl.program_id(0) == 0)
+    def _():
+        slot = lax.broadcasted_iota(jnp.int32, (total, slots), 1)
+        for h in range(hops):
+            weigh[h] = jnp.where(slot == key_ref[:, h : h + 1], gate_ref[:, h : h + 1], 0.0).astype(BF)
+
+    added = jnp.dot(weigh[0], blocks[0][...], preferred_element_type=F32)
+    for h in range(1, hops):
+        added += jnp.dot(weigh[h], blocks[h][...], preferred_element_type=F32)
+    rows = outs[0].shape[0]
+    for r, out in enumerate(outs):
+        out[...] = added[r * rows : (r + 1) * rows].astype(BF)
+
+
+def add_rows(key, gate, blocks, parts, tile=512):
+    total, hops = key.shape
+    slots, columns = blocks[0].shape
+    return pl.pallas_call(
+        add_kernel,
+        out_shape=[jax.ShapeDtypeStruct((total // parts, columns), BF)] * parts,
+        grid=(columns // tile,),
+        in_specs=[pl.BlockSpec((total, hops), lambda i: (0, 0))] * 2
+        + [pl.BlockSpec((slots, tile), lambda i: (0, i))] * hops,
+        out_specs=[pl.BlockSpec((total // parts, tile), lambda i: (0, i))] * parts,
+        scratch_shapes=[pltpu.VMEM((hops, total, slots), BF)],
+        cost_estimate=pl.CostEstimate(
+            flops=2 * hops * slots * total * columns,
+            bytes_accessed=2 * columns * (total + hops * slots),
+            transcendentals=0,
+        ),
+    )(key, gate, *blocks)
 
 
 def half_expert(rows, gate_part, up_part, down_part):
@@ -102,23 +181,14 @@
     first = jnp.concatenate(from_ring(sent[:half], "y"), axis=0)
     second = jnp.concatenate(from_ring(sent[half:], "z"), axis=0)
     first, second = lax.optimization_barrier((first, second))
-    pieces = from_ring(first, "z") + from_ring(second, "y")
+    lower, upper = along_node(first, "z", 1), along_node(first, "z", -1)
+    left, right = along_node(second, "y", 1), along_node(second, "y", -1)
+    pieces = [first, lower, upper, relayed(lower, upper, "z")]
+    pieces += [second, left, right, relayed(left, right, "y")]
     total = nodes * tok_count
-    gathered = jnp.concatenate(pieces, axis=0)
-    token_rows = gathered[:, :feature_count]
-
-    def in_order(columns):
-        one = columns[: total // 2].reshape(4, 4, half, -1)
-        two = columns[total // 2 :].reshape(4, 4, half, -1).transpose(1, 0, 2, 3)
-        return jnp.concatenate([one, two], axis=2).reshape(total, -1)
-
-    def as_rows(columns):
-        both = columns.reshape(4, 4, 2, half, -1)
-        one = both[:, :, 0].reshape(total // 2, -1)
-        two = both[:, :, 1].transpose(1, 0, 2, 3).reshape(total // 2, -1)
-        return jnp.concatenate([one, two], axis=0)
-
-    routes = in_order(gathered[:, feature_count : feature_count + 2 * top_count])
+    routes = jnp.concatenate(
+        [p[:, feature_count : feature_count + 2 * top_count] for p in pieces], axis=0
+    )
     ids = routes[:, :top_count].astype(jnp.int32)
     gates = routes[:, top_count:].astype(F32)
 
@@ -127,24 +197,17 @@
     match = ids[:, :, None] == here[None, None, :]
     routed = jnp.any(match, axis=1)
     gate_of = jnp.sum(jnp.where(match, gates[:, :, None], 0.0), axis=1)
-    before = (jnp.arange(tok_count)[:, None] > jnp.arange(tok_count)[None, :]).astype(BF)
-    position = jnp.einsum(
-        "ij,sjx->six",
-        before,
-        routed.astype(BF).reshape(nodes, tok_count, chips),
-        preferred_element_type=F32,
-    ).reshape(total, chips)
-    source = (jnp.arange(total) // tok_count)[:, None]
-    key = jnp.where(routed, source * capacity + position.astype(jnp.int32), -1)
-    key = as_rows(key)
-    gate_of = as_rows(gate_of)
+
+    row = jnp.arange(total)
+    turn, outer, inner = row // (total // 2), row // (4 * half) % 4, row // half % 4
+    source = jnp.where(turn == 0, outer * 4 + inner, inner * 4 + outer)
+    place = turn * half + row % half
+    before = (source[:, None] == source[None, :]) & (place[:, None] > place[None, :])
+    position = jnp.dot(before.astype(BF), routed.astype(BF), preferred_element_type=F32)
+    key = jnp.where(routed, source[:, None] * capacity + position.astype(jnp.int32), -1)
     slots = nodes * capacity
-    slot_range = jnp.arange(slots)
-
-    blocks = []
-    for hops in range(chips):
-        pick = (slot_range[:, None] == key[None, :, hops]).astype(BF)
-        blocks.append(jnp.dot(pick, token_rows, preferred_element_type=F32).astype(BF))
+
+    blocks = pick_rows(key.T, pieces, slots, feature_count)
     rows = [blocks[0]] + [along_x(blocks[hops], hops, chips) for hops in range(1, chips)]
     rows = jnp.concatenate(rows, axis=0)
     mine = [w[0] for w in weights]
@@ -154,22 +217,14 @@
     back = [value[:slots]] + [
         along_x(value[hops * slots : (hops + 1) * slots], -hops, chips) for hops in range(1, chips)
     ]
-    weighted = [
-        jnp.where(key[:, hops, None] == slot_range[None, :], gate_of[:, hops, None], 0.0).astype(BF)
-        for hops in range(chips)
-    ]
-    partial = jnp.dot(
-        jnp.concatenate(weighted, axis=1), jnp.concatenate(back, axis=0), preferred_element_type=F32
-    ).astype(BF)
-    one = partial[: total // 2].reshape(4, 4 * half, feature_count)
-    two = partial[total // 2 :].reshape(4, 4 * half, feature_count)
-    one = scatter_ring([one[i] for i in range(4)], "z").reshape(4, half, feature_count)
-    two = scatter_ring([two[i] for i in range(4)], "y").reshape(4, half, feature_count)
+    parts = add_rows(key, gate_of, back, 8)
+    one = scatter_ring(parts[:4], "z").reshape(4, half, feature_count)
+    two = scatter_ring(parts[4:], "y").reshape(4, half, feature_count)
     one, two = lax.optimization_barrier((one, two))
     one = scatter_ring([one[i] for i in range(4)], "y")
     two = scatter_ring([two[i] for i in range(4)], "z")
     combined = jnp.concatenate([one, two], axis=0)
-    swapped = [swap_weight(w, matching, name) for w, name in zip(weights, "gud")]
+    swapped = [swap_weight(w, matching) for w in weights]
     return (combined, *swapped)
 
 

time: 518 us -> 472 us (0.911)
  the two profiles are of different devices: /device:TPU:82 before, /device:TPU:40 now
where the time goes in v2:
time: 472 us; the launch traced here: 470 us
  waiting for transfers between devices  229 us (49%)
  starting transfers between devices  122 us (26%)
  local copies, waits for them, and re-layouts  39.5 us (8%)
  Pallas kernels  36.5 us (8%)
  matrix products  36.3 us (8%)
  other arithmetic  5.3 us (1%)
    ppermute x26, waiting for transfers between devices, along_node(): return lax.ppermute(block, 'node', pairs)  134 us
    ppermute x6, waiting for transfers between devices, along_x(): return lax.ppermute(block, 'local', pairs)  70.9 us
    all_to_all x3, starting transfers between devices, swap_weight(): lax.all_to_all(reordered, 'node', split_axis=0, concat_axis=0, tiled=True)  44.7 us
    ppermute x26, starting transfers between devices, along_node(): return lax.ppermute(block, 'node', pairs)  43 us
    all_to_all x3, starting transfers between devices, swap_weight(): lax.all_to_all(split_parts(part, nodes), 'node', split_axis=0, concat_axi...  26.3 us
    dot_general x2, matrix products, half_expert(): return jnp.dot(hidden, down_part, preferred_element_type=F32).astype(BF)  17.9 us
    gather x3, local copies, waits for them, and re-layouts, swap_weight(): reordered = jnp.take(arrived, matching, axis=0, mode='clip')  14 us
    all_to_all x3, waiting for transfers between devices, swap_weight(): lax.all_to_all(reordered, 'node', split_axis=0, concat_axis=0, tiled=True)  13.6 us
  transfers between devices with their start and end apart: 41, of which 19 were waited for; matrix products, arithmetic and copies ran while one was open for 16% of the time, Pallas kernels for 7%

profile of v2, /device:TPU:40, one launch (start us, length us, event | category | flops | bytes accessed | tf_op | source)
XLA Modules:
  0.0 470.5 jit_solution(9696732624487005955)
XLA Ops:
  3.4 2.0 collective-permute-start.3
  5.5 3.0 collective-permute-start.5
  8.5 1.6 collective-permute-start
  10.5 5.0 %collective-permute-done.3 = bf16[32,3712]{1,0:T(8,128)(2,1)S(1)} collective-permute-done((bf16[32,3712]{1,0:T(8,128)(2,1)S(1)}, bf16[32,3712]{1,0:T(8,128)(2,1)S(1)}, u32[]{:S(2)}, u32[]{:S(2)}) %collective-permute-start.3) | collective-permute-done | bytes 237600 | tf_op jit(solution)/shard_map/ppermute | solution.py:30
  15.6 2.3 collective-permute-start.2
  18.9 4.3 collective-permute-done.2
  23.3 2.6 collective-permute-start.6
  25.9 2.5 collective-permute-start.10
  28.4 8.3 %all-to-all-start = ((bf16[16,224,512]{2,1,0:T(8,128)(2,1)}), bf16[16,224,512]{2,1,0:T(8,128)(2,1)}, u32[]{:S(2)}, u32[]{:S(2)}) async-start(bf16[16,224,512]{2,1,0:T(8,128)(2,1)} %bitcast.49), calls=%async_computation | async-start | bytes 7340032 | tf_op jit(solution)/shard_map/all_to_all | solution.py:60
  36.7 11.5 %collective-permute-done.6.refs_1_ = bf16[128,3712]{1,0:T(8,128)(2,1)} collective-permute-done((bf16[128,3712]{1,0:T(8,128)(2,1)S(1)}, bf16[128,3712]{1,0:T(8,128)(2,1)}, u32[]{:S(2)}, u32[]{:S(2)}) %collective-permute-start.6) | collective-permute-done | bytes 950304 | tf_op jit(solution)/shard_map/ppermute | solution.py:30
  49.3 3.9 collective-permute-start.8
  54.9 12.1 %collective-permute-done.7.refs_2_ = bf16[128,3712]{1,0:T(8,128)(2,1)} collective-permute-done((bf16[128,3712]{1,0:T(8,128)(2,1)S(1)}, bf16[128,3712]{1,0:T(8,128)(2,1)}, u32[]{:S(2)}, u32[]{:S(2)}) %collective-permute-start.7) | collective-permute-done | bytes 950304 | tf_op jit(solution)/shard_map/ppermute | solution.py:30
  68.9 5.6 %collective-permute-start.9 = (bf16[64,3712]{1,0:T(8,128)(2,1)S(1)}, bf16[64,3712]{1,0:T(8,128)(2,1)S(1)}, u32[]{:S(2)}, u32[]{:S(2)}) collective-permute-start(bf16[64,3712]{1,0:T(8,128)(2,1)S(1)} %slice.125), channel_id=1, source_target_pairs={{0,24},{8,0},{16,8},{24,16},{32,56},{40,32},{48,40},{56,48},{64,88... | collective-permute-start | bytes 1425416 | tf_op jit(solution)/shard_map/ppermute | solution.py:30
  76.2 1.9 slice.129
  79.1 2.1 collective-permute-start.13
  81.2 11.7 %collective-permute-done.8 = bf16[64,3712]{1,0:T(8,128)(2,1)S(1)} collective-permute-done((bf16[64,3712]{1,0:T(8,128)(2,1)S(1)}, bf16[64,3712]{1,0:T(8,128)(2,1)S(1)}, u32[]{:S(2)}, u32[]{:S(2)}) %collective-permute-start.8) | collective-permute-done | bytes 475168 | tf_op jit(solution)/shard_map/ppermute | solution.py:30
  94.0 2.2 collective-permute-done.12
  97.3 10.7 %all-to-all-start.2 = ((bf16[16,224,512]{2,1,0:T(8,128)(2,1)}), bf16[16,224,512]{2,1,0:T(8,128)(2,1)}, u32[]{:S(2)}, u32[]{:S(2)}) async-start(bf16[16,224,512]{2,1,0:T(8,128)(2,1)} %bitcast.51), calls=%async_computation.2 | async-start | bytes 7340032 | tf_op jit(solution)/shard_map/all_to_all | solution.py:60
  110.3 10.6 %shard_map.111 = (bf16[192,3584]{1,0:T(8,128)(2,1)}, bf16[192,3584]{1,0:T(8,128)(2,1)}, bf16[192,3584]{1,0:T(8,128)(2,1)}, bf16[192,3584]{1,0:T(8,128)(2,1)}) custom-call(s32[4,1024]{1,0:T(4,128)} %copy.46.key_ref, bf16[128,3712]{1,0:T(8,128)(2,1)} %copy-done.5, bf16[128,3712]{1,0:T(8,128)(2,1)} %collective-permute-done.6.refs_1_, ...), custom_call_target="tpu_custom_call" | custom-call | flops 5637144576 | bytes 12845056 | tf_op jit(solution)/shard_map/pallas_call | solution.py:102
  120.9 1.6 collective-permute-start.14
  122.4 2.7 collective-permute-start.15
  125.7 1.5 collective-permute-start.16
  127.2 2.5 constant_dynamic-update-slice_fusion.15
  129.7 24.7 %collective-permute-done.14 = bf16[192,3584]{1,0:T(8,128)(2,1)S(1)} collective-permute-done((bf16[192,3584]{1,0:T(8,128)(2,1)}, bf16[192,3584]{1,0:T(8,128)(2,1)S(1)}, u32[]{:S(2)}, u32[]{:S(2)}) %collective-permute-start.14) | collective-permute-done | bytes 1376288 | tf_op jit(solution)/shard_map/ppermute | solution.py:21
  154.4 1.3 constant_dynamic-update-slice_fusion.14
  155.7 23.8 %collective-permute-done.15 = bf16[192,3584]{1,0:T(8,128)(2,1)S(1)} collective-permute-done((bf16[192,3584]{1,0:T(8,128)(2,1)}, bf16[192,3584]{1,0:T(8,128)(2,1)S(1)}, u32[]{:S(2)}, u32[]{:S(2)}) %collective-permute-start.15) | collective-permute-done | bytes 1376288 | tf_op jit(solution)/shard_map/ppermute | solution.py:21
  179.5 1.1 constant_dynamic-update-slice_fusion.13
  180.6 7.3 %all-to-all-start.4 = ((bf16[16,32,3584]{2,1,0:T(8,128)(2,1)}), bf16[16,32,3584]{2,1,0:T(8,128)(2,1)}, u32[]{:S(2)}, u32[]{:S(2)}) async-start(bf16[16,32,3584]{2,1,0:T(8,128)(2,1)} %bitcast.54), calls=%async_computation.4 | async-start | bytes 7340032 | tf_op jit(solution)/shard_map/all_to_all | solution.py:60
  187.9 1.2 constant_dynamic-update-slice_fusion.12
  189.1 6.2 %fusion.37 = f32[768,512]{1,0:T(8,128)S(1)} fusion(bf16[768,3584]{1,0:T(8,128)(2,1)} %constant_dynamic-update-slice_fusion.12, bf16[1,3584,512]{2,1,0:T(8,128)(2,1)} %param.14), kind=kOutput, calls=%fused_computation.104 | convolution fusion | flops 2818572288 | bytes 10747904 | tf_op jit(solution)/shard_map/dot_general | solution.py:158
  195.3 5.1 %fusion.39 = f32[768,512]{1,0:T(8,128)S(1)} fusion(bf16[768,3584]{1,0:T(8,128)(2,1)} %constant_dynamic-update-slice_fusion.12, bf16[1,3584,512]{2,1,0:T(8,128)(2,1)S(1)} %copy-done.2), kind=kOutput, calls=%fused_computation.106 | convolution fusion | flops 2818572288 | bytes 10747904 | tf_op jit(solution)/shard_map/dot_general | solution.py:157
  200.4 5.3 %convolution_convert_fusion.1 = bf16[768,3584]{1,0:T(8,128)(2,1)} fusion(f32[768,512]{1,0:T(8,128)S(1)} %fusion.37, f32[768,512]{1,0:T(8,128)S(1)} %fusion.39, bf16[1,512,3584]{2,1,0:T(8,128)(2,1)S(1)} %copy-done.3), kind=kOutput, calls=%fused_computation.6 | convolution fusion | flops 2823684096 | bytes 12320768 | tf_op jit(solution)/shard_map/dot_general | solution.py:160
  205.8 4.7 gather_fusion.1
  210.5 6.1 %fusion.47 = f32[768,512]{1,0:T(8,128)S(1)} fusion(bf16[768,3584]{1,0:T(8,128)(2,1)} %constant_dynamic-update-slice_fusion.12, bf16[3584,512]{1,0:T(8,128)(2,1)} %collective-permute-done.17), kind=kOutput, calls=%fused_computation.113 | convolution fusion | flops 2818572288 | bytes 10747904 | tf_op jit(solution)/shard_map/dot_general | solution.py:157
  216.5 10.5 %all-to-all-done.4 = bf16[16,32,3584]{2,1,0:T(8,128)(2,1)} async-done(((bf16[16,32,3584]{2,1,0:T(8,128)(2,1)}), bf16[16,32,3584]{2,1,0:T(8,128)(2,1)}, u32[]{:S(2)}, u32[]{:S(2)}) %all-to-all-start.4) | async-done | bytes 3670048 | tf_op jit(solution)/shard_map/all_to_all | solution.py:60
  227.0 11.6 %all-to-all-start.1 = ((bf16[16,224,512]{2,1,0:T(8,128)(2,1)}), bf16[16,224,512]{2,1,0:T(8,128)(2,1)}, u32[]{:S(2)}, u32[]{:S(2)}) async-start(bf16[16,224,512]{2,1,0:T(8,128)(2,1)} %gather_fusion.1), calls=%async_computation.1 | async-start | bytes 7340032 | tf_op jit(solution)/shard_map/all_to_all | solution.py:62
  238.6 12.5 %add_convert_fusion = bf16[768,3584]{1,0:T(8,128)(2,1)} fusion(bf16[768,3584]{1,0:T(8,128)(2,1)} %convolution_convert_fusion.1, bf16[512,3584]{1,0:T(8,128)(2,1)} %collective-permute-done.19, f32[768,512]{1,0:T(8,128)S(1)} %fusion.47, bf16[768,3584]{1,0:T(8,128)(2,1)} %constant_dynamic-update-slice_fusion.12, bf16[3584,512]{1,0:T(8,128)(2,1)} %collective-permute-done.18), kind=kOutput, calls=%fused_computation.4 | convolution fusion | flops 5653266432 | bytes 25427968 | tf_op jit(solution)/shard_map/dot_general | solution.py:160
  251.2 4.5 fusion.43
  256.4 1.4 collective-permute-start.22
  258.9 4.7 gather_fusion.2
  263.6 13.6 %all-to-all-done.1 = bf16[16,224,512]{2,1,0:T(8,128)(2,1)} async-done(((bf16[16,224,512]{2,1,0:T(8,128)(2,1)}), bf16[16,224,512]{2,1,0:T(8,128)(2,1)}, u32[]{:S(2)}, u32[]{:S(2)}) %all-to-all-start.1) | async-done | bytes 3670048 | tf_op jit(solution)/shard_map/all_to_all | solution.py:62
  277.2 11.9 %all-to-all-start.3 = ((bf16[16,224,512]{2,1,0:T(8,128)(2,1)}), bf16[16,224,512]{2,1,0:T(8,128)(2,1)}, u32[]{:S(2)}, u32[]{:S(2)}) async-start(bf16[16,224,512]{2,1,0:T(8,128)(2,1)} %gather_fusion.2), calls=%async_computation.3 | async-start | bytes 7340032 | tf_op jit(solution)/shard_map/all_to_all | solution.py:62
  289.0 1.3 collective-permute-done.21.refs_2_
  290.3 21.1 %collective-permute-done.22.refs_3_ = bf16[192,3584]{1,0:T(8,128)(2,1)} collective-permute-done((bf16[192,3584]{1,0:T(8,128)(2,1)S(1)}, bf16[192,3584]{1,0:T(8,128)(2,1)}, u32[]{:S(2)}, u32[]{:S(2)}) %collective-permute-start.22) | collective-permute-done | bytes 1376288 | tf_op jit(solution)/shard_map/ppermute | solution.py:21
  311.4 12.6 %shard_map.112 = (bf16[128,3584]{1,0:T(8,128)(2,1)}, bf16[128,3584]{1,0:T(8,128)(2,1)}, bf16[128,3584]{1,0:T(8,128)(2,1)}, bf16[128,3584]{1,0:T(8,128)(2,1)}, bf...) custom-call(s32[1024,4]{1,0:T(8,128)} %copy-done.9, ...), custom_call_target="tpu_custom_call" | custom-call | flops 5637144576 | bytes 12845056 | tf_op jit(solution)/shard_map/pallas_call | solution.py:140
  324.7 1.5 collective-permute-start.27
  326.2 3.3 collective-permute-start.28
  329.5 4.7 gather_fusion.3
  334.7 1.5 collective-permute-start.24
  336.2 10.5 %collective-permute-done.26 = bf16[128,3584]{1,0:T(8,128)(2,1)S(1)} collective-permute-done((bf16[128,3584]{1,0:T(8,128)(2,1)}, bf16[128,3584]{1,0:T(8,128)(2,1)S(1)}, u32[]{:S(2)}, u32[]{:S(2)}) %collective-permute-start.26) | collective-permute-done | bytes 917536 | tf_op jit(solution)/shard_map/ppermute | solution.py:30
  346.7 2.1 collective-permute-start.25
  348.8 18.5 %collective-permute-done.28 = bf16[128,3584]{1,0:T(8,128)(2,1)} collective-permute-done((bf16[128,3584]{1,0:T(8,128)(2,1)}, bf16[128,3584]{1,0:T(8,128)(2,1)}, u32[]{:S(2)}, u32[]{:S(2)}) %collective-permute-start.28) | collective-permute-done | bytes 917536 | tf_op jit(solution)/shard_map/ppermute | solution.py:30
  367.3 2.0 add_convert_fusion.1
  369.4 7.0 %collective-permute-done.25 = bf16[128,3584]{1,0:T(8,128)(2,1)S(1)} collective-permute-done((bf16[128,3584]{1,0:T(8,128)(2,1)}, bf16[128,3584]{1,0:T(8,128)(2,1)S(1)}, u32[]{:S(2)}, u32[]{:S(2)}) %collective-permute-start.25) | collective-permute-done | bytes 917536 | tf_op jit(solution)/shard_map/ppermute | solution.py:30
  376.8 21.3 %all-to-all-start.5 = ((bf16[16,32,3584]{2,1,0:T(8,128)(2,1)}), bf16[16,32,3584]{2,1,0:T(8,128)(2,1)}, u32[]{:S(2)}, u32[]{:S(2)}) async-start(bf16[16,32,3584]{2,1,0:T(8,128)(2,1)} %gather_fusion.3), calls=%async_computation.5 | async-start | bytes 7340032 | tf_op jit(solution)/shard_map/all_to_all | solution.py:62
  398.8 1.5 collective-permute-start.30
  400.2 3.3 collective-permute-start.31
  404.2 1.5 collective-permute-start.33
  405.7 42.4 %collective-permute-done.29 = bf16[32,3584]{1,0:T(8,128)(2,1)S(1)} collective-permute-done((bf16[32,3584]{1,0:T(8,128)(2,1)S(1)}, bf16[32,3584]{1,0:T(8,128)(2,1)S(1)}, u32[]{:S(2)}, u32[]{:S(2)}) %collective-permute-start.29) | collective-permute-done | bytes 229408 | tf_op jit(solution)/shard_map/ppermute | solution.py:30
  448.1 2.4 collective-permute-done.31
  450.7 5.6 %collective-permute-done.34 = bf16[32,3584]{1,0:T(8,128)(2,1)S(1)} collective-permute-done((bf16[32,3584]{1,0:T(8,128)(2,1)S(1)}, bf16[32,3584]{1,0:T(8,128)(2,1)S(1)}, u32[]{:S(2)}, u32[]{:S(2)}) %collective-permute-start.34) | collective-permute-done | bytes 229408 | tf_op jit(solution)/shard_map/ppermute | solution.py:30
  457.2 4.4 shard_map.113
  461.6 4.4 shard_map.114
  466.0 4.4 shard_map.115
  (123 shorter events, 22.8 us)
Async XLA Ops:
  0.6 52.6 %copy-start = (s32[64]{0:T(128)S(1)}, s32[64]{0:T(128)}, u32[]{:S(2)}) copy-start(s32[64]{0:T(128)} %param.11) | copy-start | bytes 772
  3.4 12.1 %collective-permute-start.3 = (bf16[32,3712]{1,0:T(8,128)(2,1)S(1)}, bf16[32,3712]{1,0:T(8,128)(2,1)S(1)}, u32[]{:S(2)}, u32[]{:S(2)}) collective-permute-start(bf16[32,3712]{1,0:T(8,128)(2,1)S(1)} %get-tuple-element.46), channel_id=1, source_target_pairs={{0,8},{8,16},{16,24},{24,0},{32,40},{40,48},{48,56},{56,32},{64,72... | collective-permute-start | bytes 712712 | tf_op jit(solution)/shard_map/ppermute | solution.py:30
  5.4 12.5 %collective-permute-start.4 = (bf16[32,3712]{1,0:T(8,128)(2,1)S(1)}, bf16[32,3712]{1,0:T(8,128)(2,1)S(1)}, u32[]{:S(2)}, u32[]{:S(2)}) collective-permute-start(bf16[32,3712]{1,0:T(8,128)(2,1)S(1)} %get-tuple-element.46), channel_id=1, source_target_pairs={{0,24},{8,0},{16,8},{24,16},{32,56},{40,32},{48,40},{56,48},{64,88... | collective-permute-start | bytes 712712 | tf_op jit(solution)/shard_map/ppermute | solution.py:30
  5.5 13.3 %collective-permute-start.5 = (bf16[32,3712]{1,0:T(8,128)(2,1)S(1)}, bf16[32,3712]{1,0:T(8,128)(2,1)S(1)}, u32[]{:S(2)}, u32[]{:S(2)}) collective-permute-start(bf16[32,3712]{1,0:T(8,128)(2,1)S(1)} %get-tuple-element.46), channel_id=1, source_target_pairs={{0,16},{8,24},{16,0},{24,8},{32,48},{40,56},{48,32},{56,40},{64,80... | collective-permute-start | bytes 712712 | tf_op jit(solution)/shard_map/ppermute | solution.py:30
  8.5 10.4 %collective-permute-start = (bf16[32,3712]{1,0:T(8,128)(2,1)S(1)}, bf16[32,3712]{1,0:T(8,128)(2,1)S(1)}, u32[]{:S(2)}, u32[]{:S(2)}) collective-permute-start(bf16[32,3712]{1,0:T(8,128)(2,1)S(1)} %get-tuple-element.47), channel_id=1, source_target_pairs={{0,32},{8,40},{16,48},{24,56},{32,64},{40,72},{48,80},{56,88},{64,... | collective-permute-start | bytes 712712 | tf_op jit(solution)/shard_map/ppermute | solution.py:30
  10.1 8.8 %collective-permute-start.1 = (bf16[32,3712]{1,0:T(8,128)(2,1)S(1)}, bf16[32,3712]{1,0:T(8,128)(2,1)S(1)}, u32[]{:S(2)}, u32[]{:S(2)}) collective-permute-start(bf16[32,3712]{1,0:T(8,128)(2,1)S(1)} %get-tuple-element.47), channel_id=1, source_target_pairs={{0,96},{8,104},{16,112},{24,120},{32,0},{40,8},{48,16},{56,24},{64... | collective-permute-start | bytes 712712 | tf_op jit(solution)/shard_map/ppermute | solution.py:30
  15.6 7.6 %collective-permute-start.2 = (bf16[32,3712]{1,0:T(8,128)(2,1)S(1)}, bf16[32,3712]{1,0:T(8,128)(2,1)S(1)}, u32[]{:S(2)}, u32[]{:S(2)}) collective-permute-start(bf16[32,3712]{1,0:T(8,128)(2,1)S(1)} %get-tuple-element.47), channel_id=1, source_target_pairs={{0,64},{8,72},{16,80},{24,88},{32,96},{40,104},{48,112},{56,120},{... | collective-permute-start | bytes 712712 | tf_op jit(solution)/shard_map/ppermute | solution.py:30
  18.9 35.0 %copy-start.4 = (bf16[128,3712]{1,0:T(8,128)(2,1)}, bf16[128,3712]{1,0:T(8,128)(2,1)S(1)}, u32[]{:S(2)}) copy-start(bf16[128,3712]{1,0:T(8,128)(2,1)S(1)} %pad_maximum_fusion.1.refs_4_) | copy-start | bytes 2850820
  23.3 30.6 %copy-start.5 = (bf16[128,3712]{1,0:T(8,128)(2,1)}, bf16[128,3712]{1,0:T(8,128)(2,1)S(1)}, u32[]{:S(2)}) copy-start(bf16[128,3712]{1,0:T(8,128)(2,1)S(1)} %pad_maximum_fusion.refs_0_) | copy-start | bytes 2850820
  23.3 25.0 %collective-permute-start.6 = (bf16[128,3712]{1,0:T(8,128)(2,1)S(1)}, bf16[128,3712]{1,0:T(8,128)(2,1)}, u32[]{:S(2)}, u32[]{:S(2)}) collective-permute-start(bf16[128,3712]{1,0:T(8,128)(2,1)S(1)} %pad_maximum_fusion.refs_0_), channel_id=1, source_target_pairs={{0,8},{8,16},{16,24},{24,0},{32,40},{40,48},{48,56},{56,32},{64,72... | collective-permute-start | bytes 2850824 | tf_op jit(solution)/shard_map/ppermute | solution.py:30
  25.9 41.1 %collective-permute-start.7 = (bf16[128,3712]{1,0:T(8,128)(2,1)S(1)}, bf16[128,3712]{1,0:T(8,128)(2,1)}, u32[]{:S(2)}, u32[]{:S(2)}) collective-permute-start(bf16[128,3712]{1,0:T(8,128)(2,1)S(1)} %pad_maximum_fusion.refs_0_), channel_id=1, source_target_pairs={{0,24},{8,0},{16,8},{24,16},{32,56},{40,32},{48,40},{56,48},{64,88... | collective-permute-start | bytes 2850824 | tf_op jit(solution)/shard_map/ppermute | solution.py:30
  25.9 48.6 %collective-permute-start.10 = (bf16[128,3712]{1,0:T(8,128)(2,1)S(1)}, bf16[128,3712]{1,0:T(8,128)(2,1)}, u32[]{:S(2)}, u32[]{:S(2)}) collective-permute-start(bf16[128,3712]{1,0:T(8,128)(2,1)S(1)} %pad_maximum_fusion.1.refs_4_), channel_id=1, source_target_pairs={{0,32},{8,40},{16,48},{24,56},{32,64},{40,72},{48,80},{56,88},{64,... | collective-permute-start | bytes 2850824 | tf_op jit(solution)/shard_map/ppermute | solution.py:30
  28.4 46.9 %collective-permute-start.11 = (bf16[128,3712]{1,0:T(8,128)(2,1)S(1)}, bf16[128,3712]{1,0:T(8,128)(2,1)}, u32[]{:S(2)}, u32[]{:S(2)}) collective-permute-start(bf16[128,3712]{1,0:T(8,128)(2,1)S(1)} %pad_maximum_fusion.1.refs_4_), channel_id=1, source_target_pairs={{0,96},{8,104},{16,112},{24,120},{32,0},{40,8},{48,16},{56,24},{64... | collective-permute-start | bytes 2850824 | tf_op jit(solution)/shard_map/ppermute | solution.py:30
  28.4 68.1 %all-to-all-start = ((bf16[16,224,512]{2,1,0:T(8,128)(2,1)}), bf16[16,224,512]{2,1,0:T(8,128)(2,1)}, u32[]{:S(2)}, u32[]{:S(2)}) async-start(bf16[16,224,512]{2,1,0:T(8,128)(2,1)} %bitcast.49), calls=%async_computation | async-start | bytes 7340032 | tf_op jit(solution)/shard_map/all_to_all | solution.py:60
  49.3 43.6 %collective-permute-start.8 = (bf16[64,3712]{1,0:T(8,128)(2,1)S(1)}, bf16[64,3712]{1,0:T(8,128)(2,1)S(1)}, u32[]{:S(2)}, u32[]{:S(2)}) collective-permute-start(bf16[64,3712]{1,0:T(8,128)(2,1)S(1)} %slice.124), channel_id=1, source_target_pairs={{0,8},{8,16},{16,24},{24,0},{32,40},{40,48},{48,56},{56,32},{64,72... | collective-permute-start | bytes 1425416 | tf_op jit(solution)/shard_map/ppermute | solution.py:30
  68.9 24.0 %collective-permute-start.9 = (bf16[64,3712]{1,0:T(8,128)(2,1)S(1)}, bf16[64,3712]{1,0:T(8,128)(2,1)S(1)}, u32[]{:S(2)}, u32[]{:S(2)}) collective-permute-start(bf16[64,3712]{1,0:T(8,128)(2,1)S(1)} %slice.125), channel_id=1, source_target_pairs={{0,24},{8,0},{16,8},{24,16},{32,56},{40,32},{48,40},{56,48},{64,88... | collective-permute-start | bytes 1425416 | tf_op jit(solution)/shard_map/ppermute | solution.py:30
  78.0 18.2 %collective-permute-start.12 = (bf16[64,3712]{1,0:T(8,128)(2,1)}, bf16[64,3712]{1,0:T(8,128)(2,1)S(1)}, u32[]{:S(2)}, u32[]{:S(2)}) collective-permute-start(bf16[64,3712]{1,0:T(8,128)(2,1)} %slice.129), channel_id=1, source_target_pairs={{0,32},{8,40},{16,48},{24,56},{32,64},{40,72},{48,80},{56,88},{64,... | collective-permute-start | bytes 1425416 | tf_op jit(solution)/shard_map/ppermute | solution.py:30
  79.1 17.2 %collective-permute-start.13 = (bf16[64,3712]{1,0:T(8,128)(2,1)S(1)}, bf16[64,3712]{1,0:T(8,128)(2,1)S(1)}, u32[]{:S(2)}, u32[]{:S(2)}) collective-permute-start(bf16[64,3712]{1,0:T(8,128)(2,1)S(1)} %slice.130), channel_id=1, source_target_pairs={{0,96},{8,104},{16,112},{24,120},{32,0},{40,8},{48,16},{56,24},{64... | collective-permute-start | bytes 1425416 | tf_op jit(solution)/shard_map/ppermute | solution.py:30
  92.9 1.0 copy-start.10
  96.3 1.0 copy-start.11
  97.3 83.4 %all-to-all-start.2 = ((bf16[16,224,512]{2,1,0:T(8,128)(2,1)}), bf16[16,224,512]{2,1,0:T(8,128)(2,1)}, u32[]{:S(2)}, u32[]{:S(2)}) async-start(bf16[16,224,512]{2,1,0:T(8,128)(2,1)} %bitcast.51), calls=%async_computation.2 | async-start | bytes 7340032 | tf_op jit(solution)/shard_map/all_to_all | solution.py:60
  109.5 11.4 %copy-start.9 = (s32[1024,4]{1,0:T(8,128)}, s32[1024,4]{1,0:T(8,128)S(1)}, u32[]{:S(2)}) copy-start(s32[1024,4]{1,0:T(8,128)S(1)} %fusion.7.key_ref) | copy-start | bytes 49156
  110.3 15.4 %copy-start.12 = (s32[16]{0:T(128)S(1)}, s32[16]{0:T(128)}, u32[]{:S(2)}) copy-start(s32[16]{0:T(128)} %param.12) | copy-start | bytes 196
  120.9 33.6 %collective-permute-start.14 = (bf16[192,3584]{1,0:T(8,128)(2,1)}, bf16[192,3584]{1,0:T(8,128)(2,1)S(1)}, u32[]{:S(2)}, u32[]{:S(2)}) collective-permute-start(bf16[192,3584]{1,0:T(8,128)(2,1)} %get-tuple-element.23), channel_id=1, source_target_pairs={{0,2},{1,3},{2,4},{3,5},{4,6},{5,7},{6,0},{7,1},{8,10},{9,11},{10,... | collective-permute-start | bytes 4128776 | tf_op jit(solution)/shard_map/ppermute | solution.py:21
  122.4 57.1 %collective-permute-start.15 = (bf16[192,3584]{1,0:T(8,128)(2,1)}, bf16[192,3584]{1,0:T(8,128)(2,1)S(1)}, u32[]{:S(2)}, u32[]{:S(2)}) collective-permute-start(bf16[192,3584]{1,0:T(8,128)(2,1)} %get-tuple-element.24), channel_id=1, source_target_pairs={{0,4},{1,5},{2,6},{3,7},{4,0},{5,1},{6,2},{7,3},{8,12},{9,13},{10,... | collective-permute-start | bytes 4128776 | tf_op jit(solution)/shard_map/ppermute | solution.py:21
  125.2 85.3 %collective-permute-start.17 = (bf16[3584,512]{1,0:T(8,128)(2,1)}, bf16[3584,512]{1,0:T(8,128)(2,1)}, u32[]{:S(2)}, u32[]{:S(2)}) collective-permute-start(bf16[3584,512]{1,0:T(8,128)(2,1)} %bitcast.50), channel_id=1, source_target_pairs={{0,1},{1,0},{2,3},{3,2},{4,5},{5,4},{6,7},{7,6},{8,9},{9,8},{10,11... | collective-permute-start | bytes 11010056 | tf_op jit(solution)/shard_map/ppermute | solution.py:51
  125.2 113.5 %collective-permute-start.18 = (bf16[3584,512]{1,0:T(8,128)(2,1)}, bf16[3584,512]{1,0:T(8,128)(2,1)}, u32[]{:S(2)}, u32[]{:S(2)}) collective-permute-start(bf16[3584,512]{1,0:T(8,128)(2,1)} %bitcast.52), channel_id=1, source_target_pairs={{0,1},{1,0},{2,3},{3,2},{4,5},{5,4},{6,7},{7,6},{8,9},{9,8},{10,11... | collective-permute-start | bytes 11010056 | tf_op jit(solution)/shard_map/ppermute | solution.py:51
  125.7 62.2 %collective-permute-start.16 = (bf16[192,3584]{1,0:T(8,128)(2,1)}, bf16[192,3584]{1,0:T(8,128)(2,1)S(1)}, u32[]{:S(2)}, u32[]{:S(2)}) collective-permute-start(bf16[192,3584]{1,0:T(8,128)(2,1)} %get-tuple-element.25), channel_id=1, source_target_pairs={{0,6},{1,7},{2,0},{3,1},{4,2},{5,3},{6,4},{7,5},{8,14},{9,15},{10,... | collective-permute-start | bytes 4128776 | tf_op jit(solution)/shard_map/ppermute | solution.py:21
  154.4 84.2 %collective-permute-start.19 = (bf16[512,3584]{1,0:T(8,128)(2,1)}, bf16[512,3584]{1,0:T(8,128)(2,1)}, u32[]{:S(2)}, u32[]{:S(2)}) collective-permute-start(bf16[512,3584]{1,0:T(8,128)(2,1)} %bitcast.53), channel_id=1, source_target_pairs={{0,1},{1,0},{2,3},{3,2},{4,5},{5,4},{6,7},{7,6},{8,9},{9,8},{10,11... | collective-permute-start | bytes 11010056 | tf_op jit(solution)/shard_map/ppermute | solution.py:51
  180.6 46.4 %all-to-all-start.4 = ((bf16[16,32,3584]{2,1,0:T(8,128)(2,1)}), bf16[16,32,3584]{2,1,0:T(8,128)(2,1)}, u32[]{:S(2)}, u32[]{:S(2)}) async-start(bf16[16,32,3584]{2,1,0:T(8,128)(2,1)} %bitcast.54), calls=%async_computation.4 | async-start | bytes 7340032 | tf_op jit(solution)/shard_map/all_to_all | solution.py:60
  189.1 6.2 %copy-start.2 = (bf16[1,3584,512]{2,1,0:T(8,128)(2,1)S(1)}, bf16[1,3584,512]{2,1,0:T(8,128)(2,1)}, u32[]{:S(2)}) copy-start(bf16[1,3584,512]{2,1,0:T(8,128)(2,1)} %param.13) | copy-start | bytes 11010052
  195.3 5.1 %copy-start.3 = (bf16[1,512,3584]{2,1,0:T(8,128)(2,1)S(1)}, bf16[1,512,3584]{2,1,0:T(8,128)(2,1)}, u32[]{:S(2)}) copy-start(bf16[1,512,3584]{2,1,0:T(8,128)(2,1)} %param.15) | copy-start | bytes 11010052
  227.0 50.2 %all-to-all-start.1 = ((bf16[16,224,512]{2,1,0:T(8,128)(2,1)}), bf16[16,224,512]{2,1,0:T(8,128)(2,1)}, u32[]{:S(2)}, u32[]{:S(2)}) async-start(bf16[16,224,512]{2,1,0:T(8,128)(2,1)} %gather_fusion.1), calls=%async_computation.1 | async-start | bytes 7340032 | tf_op jit(solution)/shard_map/all_to_all | solution.py:62
  255.7 33.4 %collective-permute-start.20 = (bf16[192,3584]{1,0:T(8,128)(2,1)}, bf16[192,3584]{1,0:T(8,128)(2,1)}, u32[]{:S(2)}, u32[]{:S(2)}) collective-permute-start(bf16[192,3584]{1,0:T(8,128)(2,1)} %get-tuple-element.38), channel_id=1, source_target_pairs={{0,6},{1,7},{2,0},{3,1},{4,2},{5,3},{6,4},{7,5},{8,14},{9,15},{10,... | collective-permute-start | bytes 4128776 | tf_op jit(solution)/shard_map/ppermute | solution.py:21
  255.7 34.7 %collective-permute-start.21 = (bf16[192,3584]{1,0:T(8,128)(2,1)S(1)}, bf16[192,3584]{1,0:T(8,128)(2,1)}, u32[]{:S(2)}, u32[]{:S(2)}) collective-permute-start(bf16[192,3584]{1,0:T(8,128)(2,1)S(1)} %get-tuple-element.37), channel_id=1, source_target_pairs={{0,4},{1,5},{2,6},{3,7},{4,0},{5,1},{6,2},{7,3},{8,12},{9,13},{10,... | collective-permute-start | bytes 4128776 | tf_op jit(solution)/shard_map/ppermute | solution.py:21
  256.4 55.1 %collective-permute-start.22 = (bf16[192,3584]{1,0:T(8,128)(2,1)S(1)}, bf16[192,3584]{1,0:T(8,128)(2,1)}, u32[]{:S(2)}, u32[]{:S(2)}) collective-permute-start(bf16[192,3584]{1,0:T(8,128)(2,1)S(1)} %get-tuple-element.36), channel_id=1, source_target_pairs={{0,2},{1,3},{2,4},{3,5},{4,6},{5,7},{6,0},{7,1},{8,10},{9,11},{10,... | collective-permute-start | bytes 4128776 | tf_op jit(solution)/shard_map/ppermute | solution.py:21
  277.2 99.6 %all-to-all-start.3 = ((bf16[16,224,512]{2,1,0:T(8,128)(2,1)}), bf16[16,224,512]{2,1,0:T(8,128)(2,1)}, u32[]{:S(2)}, u32[]{:S(2)}) async-start(bf16[16,224,512]{2,1,0:T(8,128)(2,1)} %gather_fusion.2), calls=%async_computation.3 | async-start | bytes 7340032 | tf_op jit(solution)/shard_map/all_to_all | solution.py:62
  324.1 22.6 %collective-permute-start.26 = (bf16[128,3584]{1,0:T(8,128)(2,1)}, bf16[128,3584]{1,0:T(8,128)(2,1)S(1)}, u32[]{:S(2)}, u32[]{:S(2)}) collective-permute-start(bf16[128,3584]{1,0:T(8,128)(2,1)} %get-tuple-element.31), channel_id=1, source_target_pairs={{0,96},{8,104},{16,112},{24,120},{32,0},{40,8},{48,16},{56,24},{64... | collective-permute-start | bytes 2752520 | tf_op jit(solution)/shard_map/ppermute | solution.py:30
  324.7 24.1 %collective-permute-start.27 = (bf16[128,3584]{1,0:T(8,128)(2,1)}, bf16[128,3584]{1,0:T(8,128)(2,1)S(1)}, u32[]{:S(2)}, u32[]{:S(2)}) collective-permute-start(bf16[128,3584]{1,0:T(8,128)(2,1)} %get-tuple-element.32), channel_id=1, source_target_pairs={{0,32},{8,40},{16,48},{24,56},{32,64},{40,72},{48,80},{56,88},{64,... | collective-permute-start | bytes 2752520 | tf_op jit(solution)/shard_map/ppermute | solution.py:30
  326.2 41.1 %copy-start.7 = (bf16[128,3584]{1,0:T(8,128)(2,1)S(1)}, bf16[128,3584]{1,0:T(8,128)(2,1)}, u32[]{:S(2)}) copy-start(bf16[128,3584]{1,0:T(8,128)(2,1)} %get-tuple-element.30) | copy-start | bytes 2752516
  326.2 41.1 %collective-permute-start.28 = (bf16[128,3584]{1,0:T(8,128)(2,1)}, bf16[128,3584]{1,0:T(8,128)(2,1)}, u32[]{:S(2)}, u32[]{:S(2)}) collective-permute-start(bf16[128,3584]{1,0:T(8,128)(2,1)} %get-tuple-element.33), channel_id=1, source_target_pairs={{0,64},{8,72},{16,80},{24,88},{32,96},{40,104},{48,112},{56,120},{... | collective-permute-start | bytes 2752520 | tf_op jit(solution)/shard_map/ppermute | solution.py:30
  334.1 42.2 %copy-start.6 = (bf16[128,3584]{1,0:T(8,128)(2,1)S(1)}, bf16[128,3584]{1,0:T(8,128)(2,1)}, u32[]{:S(2)}) copy-start(bf16[128,3584]{1,0:T(8,128)(2,1)} %get-tuple-element.26) | copy-start | bytes 2752516
  334.1 35.2 %collective-permute-start.23 = (bf16[128,3584]{1,0:T(8,128)(2,1)}, bf16[128,3584]{1,0:T(8,128)(2,1)S(1)}, u32[]{:S(2)}, u32[]{:S(2)}) collective-permute-start(bf16[128,3584]{1,0:T(8,128)(2,1)} %get-tuple-element.27), channel_id=1, source_target_pairs={{0,24},{8,0},{16,8},{24,16},{32,56},{40,32},{48,40},{56,48},{64,88... | collective-permute-start | bytes 2752520 | tf_op jit(solution)/shard_map/ppermute | solution.py:30
  334.7 34.7 %collective-permute-start.24 = (bf16[128,3584]{1,0:T(8,128)(2,1)}, bf16[128,3584]{1,0:T(8,128)(2,1)S(1)}, u32[]{:S(2)}, u32[]{:S(2)}) collective-permute-start(bf16[128,3584]{1,0:T(8,128)(2,1)} %get-tuple-element.28), channel_id=1, source_target_pairs={{0,8},{8,16},{16,24},{24,0},{32,40},{40,48},{48,56},{56,32},{64,72... | collective-permute-start | bytes 2752520 | tf_op jit(solution)/shard_map/ppermute | solution.py:30
  346.7 29.6 %collective-permute-start.25 = (bf16[128,3584]{1,0:T(8,128)(2,1)}, bf16[128,3584]{1,0:T(8,128)(2,1)S(1)}, u32[]{:S(2)}, u32[]{:S(2)}) collective-permute-start(bf16[128,3584]{1,0:T(8,128)(2,1)} %get-tuple-element.29), channel_id=1, source_target_pairs={{0,16},{8,24},{16,0},{24,8},{32,48},{40,56},{48,32},{56,40},{64,80... | collective-permute-start | bytes 2752520 | tf_op jit(solution)/shard_map/ppermute | solution.py:30
  348.8 18.5 %copy-start.8 = (bf16[128,3584]{1,0:T(8,128)(2,1)}, bf16[128,3584]{1,0:T(8,128)(2,1)S(1)}, u32[]{:S(2)}) copy-start(bf16[128,3584]{1,0:T(8,128)(2,1)S(1)} %collective-permute-done.27) | copy-start | bytes 2752516
  376.8 89.2 %all-to-all-start.5 = ((bf16[16,32,3584]{2,1,0:T(8,128)(2,1)}), bf16[16,32,3584]{2,1,0:T(8,128)(2,1)}, u32[]{:S(2)}, u32[]{:S(2)}) async-start(bf16[16,32,3584]{2,1,0:T(8,128)(2,1)} %gather_fusion.3), calls=%async_computation.5 | async-start | bytes 7340032 | tf_op jit(solution)/shard_map/all_to_all | solution.py:62
  398.1 50.0 %collective-permute-start.29 = (bf16[32,3584]{1,0:T(8,128)(2,1)S(1)}, bf16[32,3584]{1,0:T(8,128)(2,1)S(1)}, u32[]{:S(2)}, u32[]{:S(2)}) collective-permute-start(bf16[32,3584]{1,0:T(8,128)(2,1)S(1)} %get-tuple-element.40), channel_id=1, source_target_pairs={{0,96},{8,104},{16,112},{24,120},{32,0},{40,8},{48,16},{56,24},{64... | collective-permute-start | bytes 688136 | tf_op jit(solution)/shard_map/ppermute | solution.py:30
  398.8 49.3 %collective-permute-start.30 = (bf16[32,3584]{1,0:T(8,128)(2,1)S(1)}, bf16[32,3584]{1,0:T(8,128)(2,1)S(1)}, u32[]{:S(2)}, u32[]{:S(2)}) collective-permute-start(bf16[32,3584]{1,0:T(8,128)(2,1)S(1)} %get-tuple-element.42), channel_id=1, source_target_pairs={{0,32},{8,40},{16,48},{24,56},{32,64},{40,72},{48,80},{56,88},{64,... | collective-permute-start | bytes 688136 | tf_op jit(solution)/shard_map/ppermute | solution.py:30
  400.2 50.3 %collective-permute-start.31 = (bf16[32,3584]{1,0:T(8,128)(2,1)S(1)}, bf16[32,3584]{1,0:T(8,128)(2,1)S(1)}, u32[]{:S(2)}, u32[]{:S(2)}) collective-permute-start(bf16[32,3584]{1,0:T(8,128)(2,1)S(1)} %get-tuple-element.41), channel_id=1, source_target_pairs={{0,64},{8,72},{16,80},{24,88},{32,96},{40,104},{48,112},{56,120},{... | collective-permute-start | bytes 688136 | tf_op jit(solution)/shard_map/ppermute | solution.py:30
  403.6 47.1 %collective-permute-start.32 = (bf16[32,3584]{1,0:T(8,128)(2,1)S(1)}, bf16[32,3584]{1,0:T(8,128)(2,1)S(1)}, u32[]{:S(2)}, u32[]{:S(2)}) collective-permute-start(bf16[32,3584]{1,0:T(8,128)(2,1)S(1)} %get-tuple-element.43), channel_id=1, source_target_pairs={{0,24},{8,0},{16,8},{24,16},{32,56},{40,32},{48,40},{56,48},{64,88... | collective-permute-start | bytes 688136 | tf_op jit(solution)/shard_map/ppermute | solution.py:30
  404.2 46.5 %collective-permute-start.33 = (bf16[32,3584]{1,0:T(8,128)(2,1)S(1)}, bf16[32,3584]{1,0:T(8,128)(2,1)S(1)}, u32[]{:S(2)}, u32[]{:S(2)}) collective-permute-start(bf16[32,3584]{1,0:T(8,128)(2,1)S(1)} %get-tuple-element.45), channel_id=1, source_target_pairs={{0,8},{8,16},{16,24},{24,0},{32,40},{40,48},{48,56},{56,32},{64,72... | collective-permute-start | bytes 688136 | tf_op jit(solution)/shard_map/ppermute | solution.py:30
  448.1 8.2 %collective-permute-start.34 = (bf16[32,3584]{1,0:T(8,128)(2,1)S(1)}, bf16[32,3584]{1,0:T(8,128)(2,1)S(1)}, u32[]{:S(2)}, u32[]{:S(2)}) collective-permute-start(bf16[32,3584]{1,0:T(8,128)(2,1)S(1)} %get-tuple-element.44), channel_id=1, source_target_pairs={{0,16},{8,24},{16,0},{24,8},{32,48},{40,56},{48,32},{56,40},{64,80... | collective-permute-start | bytes 688136 | tf_op jit(solution)/shard_map/ppermute | solution.py:30
  466.0 4.4 copy-start.1

commit v3 on v2

--- a/solution.py
+++ b/solution.py
@@ -208,15 +208,20 @@
     slots = nodes * capacity
 
     blocks = pick_rows(key.T, pieces, slots, feature_count)
-    rows = [blocks[0]] + [along_x(blocks[hops], hops, chips) for hops in range(1, chips)]
-    rows = jnp.concatenate(rows, axis=0)
     mine = [w[0] for w in weights]
     others = [other_core(w) for w in mine]
-    own = half_expert(rows, *mine)
-    value = (own.astype(F32) + half_expert(rows, *others).astype(F32)).astype(BF)
-    back = [value[:slots]] + [
-        along_x(value[hops * slots : (hops + 1) * slots], -hops, chips) for hops in range(1, chips)
-    ]
+
+    def expert(rows):
+        own = half_expert(rows, *mine)
+        return (own.astype(F32) + half_expert(rows, *others).astype(F32)).astype(BF)
+
+    right, left = along_x(blocks[1], 1, chips), along_x(blocks[3], 3, chips)
+    across = along_x(blocks[2], 2, chips)
+    value = expert(jnp.concatenate([right, left], axis=0))
+    right, left = along_x(value[:slots], -1, chips), along_x(value[slots:], -3, chips)
+    value = expert(jnp.concatenate([blocks[0], across], axis=0))
+    across = along_x(value[slots:], -2, chips)
+    back = [value[:slots], right, across, left]
     parts = add_rows(key, gate_of, back, 8)
     one = scatter_ring(parts[:4], "z").reshape(4, half, feature_count)
     two = scatter_ring(parts[4:], "y").reshape(4, half, feature_count)

time: 472 us -> 480 us (1.017)
  the two profiles are of different devices: /device:TPU:40 before, /device:TPU:58 now
where the time goes in v3:
time: 480 us; the launch traced here: 474 us
  waiting for transfers between devices  250 us (52%)
  starting transfers between devices  93.5 us (19%)
  matrix products  50.3 us (10%)
  local copies, waits for them, and re-layouts  36.9 us (8%)
  Pallas kernels  36.5 us (8%)
  other arithmetic  5.3 us (1%)
    ppermute x26, waiting for transfers between devices, along_node(): return lax.ppermute(block, 'node', pairs)  179 us
    ppermute x6, waiting for transfers between devices, along_x(): return lax.ppermute(block, 'local', pairs)  43.9 us
    dot_general x4, matrix products, half_expert(): return jnp.dot(hidden, down_part, preferred_element_type=F32).astype(BF)  36.1 us
    ppermute x26, starting transfers between devices, along_node(): return lax.ppermute(block, 'node', pairs)  34 us
    all_to_all x3, starting transfers between devices, swap_weight(): lax.all_to_all(split_parts(part, nodes), 'node', split_axis=0, concat_axi...  24.6 us
    all_to_all x3, starting transfers between devices, swap_weight(): lax.all_to_all(reordered, 'node', split_axis=0, concat_axis=0, tiled=True)  22.5 us
    all_to_all x3, waiting for transfers between devices, swap_weight(): lax.all_to_all(reordered, 'node', split_axis=0, concat_axis=0, tiled=True)  22.2 us
    gather x3, local copies, waits for them, and re-layouts, swap_weight(): reordered = jnp.take(arrived, matching, axis=0, mode='clip')  14.2 us
  transfers between devices with their start and end apart: 41, of which 18 were waited for; matrix products, arithmetic and copies ran while one was open for 18% of the time, Pallas kernels for 7%

profile of v3, /device:TPU:58, one launch (start us, length us, event | category | flops | bytes accessed | tf_op | source)
XLA Modules:
  0.0 474.1 jit_solution(13857256631586329666)
XLA Ops:
  2.2 1.1 concatenate.27
  3.4 2.0 collective-permute-start.3
  5.5 3.0 collective-permute-start.5
  8.7 1.8 collective-permute-start.1
  10.5 5.0 %collective-permute-done.3 = bf16[32,3712]{1,0:T(8,128)(2,1)S(1)} collective-permute-done((bf16[32,3712]{1,0:T(8,128)(2,1)S(1)}, bf16[32,3712]{1,0:T(8,128)(2,1)S(1)}, u32[]{:S(2)}, u32[]{:S(2)}) %collective-permute-start.3) | collective-permute-done | bytes 237600 | tf_op jit(solution)/shard_map/ppermute | solution.py:30
  15.6 1.2 collective-permute-start.2
  16.8 2.0 collective-permute-done.5
  18.9 4.2 collective-permute-done.2
  23.3 2.5 collective-permute-start.6
  26.2 1.6 collective-permute-start.11
  27.8 8.7 %all-to-all-start = ((bf16[16,224,512]{2,1,0:T(8,128)(2,1)}), bf16[16,224,512]{2,1,0:T(8,128)(2,1)}, u32[]{:S(2)}, u32[]{:S(2)}) async-start(bf16[16,224,512]{2,1,0:T(8,128)(2,1)} %bitcast.70), calls=%async_computation | async-start | bytes 7340032 | tf_op jit(solution)/shard_map/all_to_all | solution.py:60
  36.5 12.6 %collective-permute-done.6.refs_1_ = bf16[128,3712]{1,0:T(8,128)(2,1)} collective-permute-done((bf16[128,3712]{1,0:T(8,128)(2,1)S(1)}, bf16[128,3712]{1,0:T(8,128)(2,1)}, u32[]{:S(2)}, u32[]{:S(2)}) %collective-permute-start.6) | collective-permute-done | bytes 950304 | tf_op jit(solution)/shard_map/ppermute | solution.py:30
  50.2 6.2 %collective-permute-start.8 = (bf16[64,3712]{1,0:T(8,128)(2,1)S(1)}, bf16[64,3712]{1,0:T(8,128)(2,1)S(1)}, u32[]{:S(2)}, u32[]{:S(2)}) collective-permute-start(bf16[64,3712]{1,0:T(8,128)(2,1)S(1)} %slice.124), channel_id=1, source_target_pairs={{0,8},{8,16},{16,24},{24,0},{32,40},{40,48},{48,56},{56,32},{64,72... | collective-permute-start | bytes 1425416 | tf_op jit(solution)/shard_map/ppermute | solution.py:30
  58.1 5.8 %collective-permute-done.7.refs_2_ = bf16[128,3712]{1,0:T(8,128)(2,1)} collective-permute-done((bf16[128,3712]{1,0:T(8,128)(2,1)S(1)}, bf16[128,3712]{1,0:T(8,128)(2,1)}, u32[]{:S(2)}, u32[]{:S(2)}) %collective-permute-start.7) | collective-permute-done | bytes 950304 | tf_op jit(solution)/shard_map/ppermute | solution.py:30
  64.7 1.1 slice.125
  68.1 1.9 slice.129
  71.0 2.1 collective-permute-start.13
  73.1 20.4 %collective-permute-done.8 = bf16[64,3712]{1,0:T(8,128)(2,1)S(1)} collective-permute-done((bf16[64,3712]{1,0:T(8,128)(2,1)S(1)}, bf16[64,3712]{1,0:T(8,128)(2,1)S(1)}, u32[]{:S(2)}, u32[]{:S(2)}) %collective-permute-start.8) | collective-permute-done | bytes 475168 | tf_op jit(solution)/shard_map/ppermute | solution.py:30
  95.8 3.6 collective-permute-done.13
  100.0 1.1 fusion.15.key_ref
  101.8 10.6 %shard_map.111 = (bf16[192,3584]{1,0:T(8,128)(2,1)}, bf16[192,3584]{1,0:T(8,128)(2,1)}, bf16[192,3584]{1,0:T(8,128)(2,1)}, bf16[192,3584]{1,0:T(8,128)(2,1)}) custom-call(s32[4,1024]{1,0:T(4,128)} %copy.46.key_ref, bf16[128,3712]{1,0:T(8,128)(2,1)} %copy-done.5, bf16[128,3712]{1,0:T(8,128)(2,1)} %collective-permute-done.6.refs_1_, ...), custom_call_target="tpu_custom_call" | custom-call | flops 5637144576 | bytes 12845056 | tf_op jit(solution)/shard_map/pallas_call | solution.py:102
  112.5 1.6 collective-permute-start.18
  115.1 2.2 collective-permute-start.14
  117.3 7.5 %all-to-all-start.2 = ((bf16[16,224,512]{2,1,0:T(8,128)(2,1)}), bf16[16,224,512]{2,1,0:T(8,128)(2,1)}, u32[]{:S(2)}, u32[]{:S(2)}) async-start(bf16[16,224,512]{2,1,0:T(8,128)(2,1)} %bitcast.73), calls=%async_computation.2 | async-start | bytes 7340032 | tf_op jit(solution)/shard_map/all_to_all | solution.py:60
  124.9 21.0 %collective-permute-done.18 = bf16[192,3584]{1,0:T(8,128)(2,1)} collective-permute-done((bf16[192,3584]{1,0:T(8,128)(2,1)}, bf16[192,3584]{1,0:T(8,128)(2,1)}, u32[]{:S(2)}, u32[]{:S(2)}) %collective-permute-start.18) | collective-permute-done | bytes 1376288 | tf_op jit(solution)/shard_map/ppermute | solution.py:21
  145.9 1.4 constant_dynamic-update-slice_fusion.15
  147.5 22.9 %collective-permute-done.14 = bf16[192,3584]{1,0:T(8,128)(2,1)} collective-permute-done((bf16[192,3584]{1,0:T(8,128)(2,1)}, bf16[192,3584]{1,0:T(8,128)(2,1)}, u32[]{:S(2)}, u32[]{:S(2)}) %collective-permute-start.14) | collective-permute-done | bytes 1376288 | tf_op jit(solution)/shard_map/ppermute | solution.py:21
  170.4 1.4 constant_dynamic-update-slice_fusion.12
  171.8 1.6 fusion.60
  173.4 2.5 fusion.62
  175.9 9.5 %fusion.4 = f32[384,3584]{1,0:T(8,128)} fusion(f32[384,512]{1,0:T(8,128)S(1)} %fusion.60, bf16[1,512,3584]{2,1,0:T(8,128)(2,1)} %param.15, bf16[384,3584]{1,0:T(8,128)(2,1)} %copy-done.12, bf16[1,3584,512]{2,1,0:T(8,128)(2,1)} %param.14), kind=kOutput, calls=%fused_computation.12 | convolution fusion | flops 2822504448 | bytes 16384000 | tf_op jit(solution)/shard_map/dot_general | solution.py:160
  185.4 8.4 %all-to-all-start.4 = ((bf16[16,32,3584]{2,1,0:T(8,128)(2,1)}), bf16[16,32,3584]{2,1,0:T(8,128)(2,1)}, u32[]{:S(2)}, u32[]{:S(2)}) async-start(bf16[16,32,3584]{2,1,0:T(8,128)(2,1)} %bitcast.75), calls=%async_computation.4 | async-start | bytes 7340032 | tf_op jit(solution)/shard_map/all_to_all | solution.py:60
  193.8 9.0 %fusion = f32[384,3584]{1,0:T(8,128)} fusion(f32[384,512]{1,0:T(8,128)} %fusion.62, bf16[1,512,3584]{2,1,0:T(8,128)(2,1)} %param.15, bf16[384,3584]{1,0:T(8,128)(2,1)S(1)} %copy-done.10, bf16[1,3584,512]{2,1,0:T(8,128)(2,1)} %param.14), kind=kOutput, calls=%fused_computation.8 | convolution fusion | flops 2822504448 | bytes 16384000 | tf_op jit(solution)/shard_map/dot_general | solution.py:160
  202.7 4.8 %gather_fusion.1 = bf16[16,224,512]{2,1,0:T(8,128)(2,1)} fusion(bf16[16,224,512]{2,1,0:T(8,128)(2,1)} %all-to-all-done, s32[1024]{0:T(1024)S(1)} %pad_clamp_fusion), kind=kCustom, calls=%fused_computation.1 | custom fusion | bytes 7340096 | tf_op jit(solution)/shard_map/jit(_take)/gather | solution.py:61
  207.5 4.5 fusion.76
  212.1 8.8 %fusion.7 = bf16[384,3584]{1,0:T(8,128)(2,1)S(1)} fusion(f32[384,3584]{1,0:T(8,128)} %fusion.4, bf16[512,3584]{1,0:T(8,128)(2,1)} %collective-permute-done.17, f32[384,512]{1,0:T(8,128)} %fusion.76, bf16[384,3584]{1,0:T(8,128)(2,1)} %copy-done.12, bf16[3584,512]{1,0:T(8,128)(2,1)} %collective-permute-done.16), kind=kOutput, calls=%fused_computation.15 | convolution fusion | flops 2825256960 | bytes 19136512 | tf_op jit(solution)/shard_map/dot_general | solution.py:160
  220.9 1.7 fusion.68
  223.5 1.1 collective-permute-start.22
  224.7 4.5 fusion.75
  229.2 5.6 %all-to-all-done.4 = bf16[16,32,3584]{2,1,0:T(8,128)(2,1)} async-done(((bf16[16,32,3584]{2,1,0:T(8,128)(2,1)}), bf16[16,32,3584]{2,1,0:T(8,128)(2,1)}, u32[]{:S(2)}, u32[]{:S(2)}) %all-to-all-start.4) | async-done | bytes 3670048 | tf_op jit(solution)/shard_map/all_to_all | solution.py:60
  234.8 8.4 %all-to-all-start.1 = ((bf16[16,224,512]{2,1,0:T(8,128)(2,1)}), bf16[16,224,512]{2,1,0:T(8,128)(2,1)}, u32[]{:S(2)}, u32[]{:S(2)}) async-start(bf16[16,224,512]{2,1,0:T(8,128)(2,1)} %gather_fusion.1), calls=%async_computation.1 | async-start | bytes 7340032 | tf_op jit(solution)/shard_map/all_to_all | solution.py:62
  243.2 8.8 %fusion.3 = bf16[384,3584]{1,0:T(8,128)(2,1)S(1)} fusion(f32[384,3584]{1,0:T(8,128)} %fusion, bf16[512,3584]{1,0:T(8,128)(2,1)} %collective-permute-done.17, f32[384,512]{1,0:T(8,128)} %fusion.75, bf16[384,3584]{1,0:T(8,128)(2,1)} %copy-done.9, bf16[3584,512]{1,0:T(8,128)(2,1)} %collective-permute-done.16), kind=kOutput, calls=%fused_computation.11 | convolution fusion | flops 2825256960 | bytes 19136512 | tf_op jit(solution)/shard_map/dot_general | solution.py:160
  252.1 1.7 fusion.69
  253.8 5.6 %collective-permute-start.21 = (bf16[192,3584]{1,0:T(8,128)(2,1)}, bf16[192,3584]{1,0:T(8,128)(2,1)S(1)}, u32[]{:S(2)}, u32[]{:S(2)}) collective-permute-start(bf16[192,3584]{1,0:T(8,128)(2,1)} %get-tuple-element.38), channel_id=1, source_target_pairs={{0,4},{1,5},{2,6},{3,7},{4,0},{5,1},{6,2},{7,3},{8,12},{9,13},{10,... | collective-permute-start | bytes 4128776 | tf_op jit(solution)/shard_map/ppermute | solution.py:21
  260.6 4.7 gather_fusion.2
  265.2 22.2 %all-to-all-done.1 = bf16[16,224,512]{2,1,0:T(8,128)(2,1)} async-done(((bf16[16,224,512]{2,1,0:T(8,128)(2,1)}), bf16[16,224,512]{2,1,0:T(8,128)(2,1)}, u32[]{:S(2)}, u32[]{:S(2)}) %all-to-all-start.1) | async-done | bytes 3670048 | tf_op jit(solution)/shard_map/all_to_all | solution.py:62
  287.4 8.7 %all-to-all-start.3 = ((bf16[16,224,512]{2,1,0:T(8,128)(2,1)}), bf16[16,224,512]{2,1,0:T(8,128)(2,1)}, u32[]{:S(2)}, u32[]{:S(2)}) async-start(bf16[16,224,512]{2,1,0:T(8,128)(2,1)} %gather_fusion.2), calls=%async_computation.3 | async-start | bytes 7340032 | tf_op jit(solution)/shard_map/all_to_all | solution.py:62
  296.1 1.1 copy-done.18
  297.2 12.7 %shard_map.112 = (bf16[128,3584]{1,0:T(8,128)(2,1)}, bf16[128,3584]{1,0:T(8,128)(2,1)}, bf16[128,3584]{1,0:T(8,128)(2,1)}, bf16[128,3584]{1,0:T(8,128)(2,1)}, bf...) custom-call(s32[1024,4]{1,0:T(8,128)} %copy-done.14, ...), custom_call_target="tpu_custom_call" | custom-call | flops 5637144576 | bytes 12845056 | tf_op jit(solution)/shard_map/pallas_call | solution.py:140
  310.8 2.4 collective-permute-start.27
  313.4 4.7 gather_fusion.3
  318.7 1.5 collective-permute-start.24
  320.1 55.8 %collective-permute-done.26 = bf16[128,3584]{1,0:T(8,128)(2,1)S(1)} collective-permute-done((bf16[128,3584]{1,0:T(8,128)(2,1)}, bf16[128,3584]{1,0:T(8,128)(2,1)S(1)}, u32[]{:S(2)}, u32[]{:S(2)}) %collective-permute-start.26) | collective-permute-done | bytes 917536 | tf_op jit(solution)/shard_map/ppermute | solution.py:30
  377.0 2.0 add_convert_fusion
  379.0 20.1 %collective-permute-done.25 = bf16[128,3584]{1,0:T(8,128)(2,1)S(1)} collective-permute-done((bf16[128,3584]{1,0:T(8,128)(2,1)}, bf16[128,3584]{1,0:T(8,128)(2,1)S(1)}, u32[]{:S(2)}, u32[]{:S(2)}) %collective-permute-start.25) | collective-permute-done | bytes 917536 | tf_op jit(solution)/shard_map/ppermute | solution.py:30
  399.5 5.4 %all-to-all-start.5 = ((bf16[16,32,3584]{2,1,0:T(8,128)(2,1)}), bf16[16,32,3584]{2,1,0:T(8,128)(2,1)}, u32[]{:S(2)}, u32[]{:S(2)}) async-start(bf16[16,32,3584]{2,1,0:T(8,128)(2,1)} %gather_fusion.3), calls=%async_computation.5 | async-start | bytes 7340032 | tf_op jit(solution)/shard_map/all_to_all | solution.py:62
  405.9 2.4 collective-permute-start.30
  409.3 1.5 collective-permute-start.33
  410.7 41.6 %collective-permute-done.29 = bf16[32,3584]{1,0:T(8,128)(2,1)S(1)} collective-permute-done((bf16[32,3584]{1,0:T(8,128)(2,1)S(1)}, bf16[32,3584]{1,0:T(8,128)(2,1)S(1)}, u32[]{:S(2)}, u32[]{:S(2)}) %collective-permute-start.29) | collective-permute-done | bytes 229408 | tf_op jit(solution)/shard_map/ppermute | solution.py:30
  453.7 1.1 collective-permute-done.31
  455.0 4.9 %collective-permute-done.34 = bf16[32,3584]{1,0:T(8,128)(2,1)S(1)} collective-permute-done((bf16[32,3584]{1,0:T(8,128)(2,1)S(1)}, bf16[32,3584]{1,0:T(8,128)(2,1)S(1)}, u32[]{:S(2)}, u32[]{:S(2)}) %collective-permute-start.34) | collective-permute-done | bytes 229408 | tf_op jit(solution)/shard_map/ppermute | solution.py:30
  460.8 4.4 shard_map.113
  465.2 4.4 shard_map.114
  469.6 4.4 shard_map.115
  (139 shorter events, 23.8 us)
Async XLA Ops:
  0.6 55.8 %copy-start = (s32[64]{0:T(128)S(1)}, s32[64]{0:T(128)}, u32[]{:S(2)}) copy-start(s32[64]{0:T(128)} %param.11) | copy-start | bytes 772
  3.4 12.1 %collective-permute-start.3 = (bf16[32,3712]{1,0:T(8,128)(2,1)S(1)}, bf16[32,3712]{1,0:T(8,128)(2,1)S(1)}, u32[]{:S(2)}, u32[]{:S(2)}) collective-permute-start(bf16[32,3712]{1,0:T(8,128)(2,1)S(1)} %get-tuple-element.46), channel_id=1, source_target_pairs={{0,8},{8,16},{16,24},{24,0},{32,40},{40,48},{48,56},{56,32},{64,72... | collective-permute-start | bytes 712712 | tf_op jit(solution)/shard_map/ppermute | solution.py:30
  5.4 11.4 %collective-permute-start.4 = (bf16[32,3712]{1,0:T(8,128)(2,1)S(1)}, bf16[32,3712]{1,0:T(8,128)(2,1)S(1)}, u32[]{:S(2)}, u32[]{:S(2)}) collective-permute-start(bf16[32,3712]{1,0:T(8,128)(2,1)S(1)} %get-tuple-element.46), channel_id=1, source_target_pairs={{0,24},{8,0},{16,8},{24,16},{32,56},{40,32},{48,40},{56,48},{64,88... | collective-permute-start | bytes 712712 | tf_op jit(solution)/shard_map/ppermute | solution.py:30
  5.5 13.3 %collective-permute-start.5 = (bf16[32,3712]{1,0:T(8,128)(2,1)S(1)}, bf16[32,3712]{1,0:T(8,128)(2,1)S(1)}, u32[]{:S(2)}, u32[]{:S(2)}) collective-permute-start(bf16[32,3712]{1,0:T(8,128)(2,1)S(1)} %get-tuple-element.46), channel_id=1, source_target_pairs={{0,16},{8,24},{16,0},{24,8},{32,48},{40,56},{48,32},{56,40},{64,80... | collective-permute-start | bytes 712712 | tf_op jit(solution)/shard_map/ppermute | solution.py:30
  8.5 10.4 %collective-permute-start = (bf16[32,3712]{1,0:T(8,128)(2,1)S(1)}, bf16[32,3712]{1,0:T(8,128)(2,1)S(1)}, u32[]{:S(2)}, u32[]{:S(2)}) collective-permute-start(bf16[32,3712]{1,0:T(8,128)(2,1)S(1)} %get-tuple-element.47), channel_id=1, source_target_pairs={{0,32},{8,40},{16,48},{24,56},{32,64},{40,72},{48,80},{56,88},{64,... | collective-permute-start | bytes 712712 | tf_op jit(solution)/shard_map/ppermute | solution.py:30
  8.7 10.2 %collective-permute-start.1 = (bf16[32,3712]{1,0:T(8,128)(2,1)S(1)}, bf16[32,3712]{1,0:T(8,128)(2,1)S(1)}, u32[]{:S(2)}, u32[]{:S(2)}) collective-permute-start(bf16[32,3712]{1,0:T(8,128)(2,1)S(1)} %get-tuple-element.47), channel_id=1, source_target_pairs={{0,96},{8,104},{16,112},{24,120},{32,0},{40,8},{48,16},{56,24},{64... | collective-permute-start | bytes 712712 | tf_op jit(solution)/shard_map/ppermute | solution.py:30
  15.6 7.6 %collective-permute-start.2 = (bf16[32,3712]{1,0:T(8,128)(2,1)S(1)}, bf16[32,3712]{1,0:T(8,128)(2,1)S(1)}, u32[]{:S(2)}, u32[]{:S(2)}) collective-permute-start(bf16[32,3712]{1,0:T(8,128)(2,1)S(1)} %get-tuple-element.47), channel_id=1, source_target_pairs={{0,64},{8,72},{16,80},{24,88},{32,96},{40,104},{48,112},{56,120},{... | collective-permute-start | bytes 712712 | tf_op jit(solution)/shard_map/ppermute | solution.py:30
  18.9 38.2 %copy-start.4 = (bf16[128,3712]{1,0:T(8,128)(2,1)}, bf16[128,3712]{1,0:T(8,128)(2,1)S(1)}, u32[]{:S(2)}) copy-start(bf16[128,3712]{1,0:T(8,128)(2,1)S(1)} %pad_maximum_fusion.1.refs_4_) | copy-start | bytes 2850820
  23.3 33.8 %copy-start.5 = (bf16[128,3712]{1,0:T(8,128)(2,1)}, bf16[128,3712]{1,0:T(8,128)(2,1)S(1)}, u32[]{:S(2)}) copy-start(bf16[128,3712]{1,0:T(8,128)(2,1)S(1)} %pad_maximum_fusion.refs_0_) | copy-start | bytes 2850820
  23.3 25.8 %collective-permute-start.6 = (bf16[128,3712]{1,0:T(8,128)(2,1)S(1)}, bf16[128,3712]{1,0:T(8,128)(2,1)}, u32[]{:S(2)}, u32[]{:S(2)}) collective-permute-start(bf16[128,3712]{1,0:T(8,128)(2,1)S(1)} %pad_maximum_fusion.refs_0_), channel_id=1, source_target_pairs={{0,8},{8,16},{16,24},{24,0},{32,40},{40,48},{48,56},{56,32},{64,72... | collective-permute-start | bytes 2850824 | tf_op jit(solution)/shard_map/ppermute | solution.py:30
  25.8 38.1 %collective-permute-start.7 = (bf16[128,3712]{1,0:T(8,128)(2,1)S(1)}, bf16[128,3712]{1,0:T(8,128)(2,1)}, u32[]{:S(2)}, u32[]{:S(2)}) collective-permute-start(bf16[128,3712]{1,0:T(8,128)(2,1)S(1)} %pad_maximum_fusion.refs_0_), channel_id=1, source_target_pairs={{0,24},{8,0},{16,8},{24,16},{32,56},{40,32},{48,40},{56,48},{64,88... | collective-permute-start | bytes 2850824 | tf_op jit(solution)/shard_map/ppermute | solution.py:30
  25.8 40.6 %collective-permute-start.10 = (bf16[128,3712]{1,0:T(8,128)(2,1)S(1)}, bf16[128,3712]{1,0:T(8,128)(2,1)}, u32[]{:S(2)}, u32[]{:S(2)}) collective-permute-start(bf16[128,3712]{1,0:T(8,128)(2,1)S(1)} %pad_maximum_fusion.1.refs_4_), channel_id=1, source_target_pairs={{0,32},{8,40},{16,48},{24,56},{32,64},{40,72},{48,80},{56,88},{64,... | collective-permute-start | bytes 2850824 | tf_op jit(solution)/shard_map/ppermute | solution.py:30
  26.2 41.0 %collective-permute-start.11 = (bf16[128,3712]{1,0:T(8,128)(2,1)S(1)}, bf16[128,3712]{1,0:T(8,128)(2,1)}, u32[]{:S(2)}, u32[]{:S(2)}) collective-permute-start(bf16[128,3712]{1,0:T(8,128)(2,1)S(1)} %pad_maximum_fusion.1.refs_4_), channel_id=1, source_target_pairs={{0,96},{8,104},{16,112},{24,120},{32,0},{40,8},{48,16},{56,24},{64... | collective-permute-start | bytes 2850824 | tf_op jit(solution)/shard_map/ppermute | solution.py:30
  27.8 89.5 %all-to-all-start = ((bf16[16,224,512]{2,1,0:T(8,128)(2,1)}), bf16[16,224,512]{2,1,0:T(8,128)(2,1)}, u32[]{:S(2)}, u32[]{:S(2)}) async-start(bf16[16,224,512]{2,1,0:T(8,128)(2,1)} %bitcast.70), calls=%async_computation | async-start | bytes 7340032 | tf_op jit(solution)/shard_map/all_to_all | solution.py:60
  50.2 43.4 %collective-permute-start.8 = (bf16[64,3712]{1,0:T(8,128)(2,1)S(1)}, bf16[64,3712]{1,0:T(8,128)(2,1)S(1)}, u32[]{:S(2)}, u32[]{:S(2)}) collective-permute-start(bf16[64,3712]{1,0:T(8,128)(2,1)S(1)} %slice.124), channel_id=1, source_target_pairs={{0,8},{8,16},{16,24},{24,0},{32,40},{40,48},{48,56},{56,32},{64,72... | collective-permute-start | bytes 1425416 | tf_op jit(solution)/shard_map/ppermute | solution.py:30
  65.8 27.8 %collective-permute-start.9 = (bf16[64,3712]{1,0:T(8,128)(2,1)S(1)}, bf16[64,3712]{1,0:T(8,128)(2,1)S(1)}, u32[]{:S(2)}, u32[]{:S(2)}) collective-permute-start(bf16[64,3712]{1,0:T(8,128)(2,1)S(1)} %slice.125), channel_id=1, source_target_pairs={{0,24},{8,0},{16,8},{24,16},{32,56},{40,32},{48,40},{56,48},{64,88... | collective-permute-start | bytes 1425416 | tf_op jit(solution)/shard_map/ppermute | solution.py:30
  69.9 25.8 %collective-permute-start.12 = (bf16[64,3712]{1,0:T(8,128)(2,1)}, bf16[64,3712]{1,0:T(8,128)(2,1)S(1)}, u32[]{:S(2)}, u32[]{:S(2)}) collective-permute-start(bf16[64,3712]{1,0:T(8,128)(2,1)} %slice.129), channel_id=1, source_target_pairs={{0,32},{8,40},{16,48},{24,56},{32,64},{40,72},{48,80},{56,88},{64,... | collective-permute-start | bytes 1425416 | tf_op jit(solution)/shard_map/ppermute | solution.py:30
  71.0 28.3 %collective-permute-start.13 = (bf16[64,3712]{1,0:T(8,128)(2,1)S(1)}, bf16[64,3712]{1,0:T(8,128)(2,1)S(1)}, u32[]{:S(2)}, u32[]{:S(2)}) collective-permute-start(bf16[64,3712]{1,0:T(8,128)(2,1)S(1)} %slice.130), channel_id=1, source_target_pairs={{0,96},{8,104},{16,112},{24,120},{32,0},{40,8},{48,16},{56,24},{64... | collective-permute-start | bytes 1425416 | tf_op jit(solution)/shard_map/ppermute | solution.py:30
  93.6 1.0 copy-start.15
  99.4 2.5 copy-start.16
  101.0 11.4 %copy-start.14 = (s32[1024,4]{1,0:T(8,128)}, s32[1024,4]{1,0:T(8,128)S(1)}, u32[]{:S(2)}) copy-start(s32[1024,4]{1,0:T(8,128)S(1)} %fusion.15.key_ref) | copy-start | bytes 49156
  101.8 13.2 %copy-start.17 = (s32[16]{0:T(128)S(1)}, s32[16]{0:T(128)}, u32[]{:S(2)}) copy-start(s32[16]{0:T(128)} %param.12) | copy-start | bytes 196
  112.5 33.4 %collective-permute-start.18 = (bf16[192,3584]{1,0:T(8,128)(2,1)}, bf16[192,3584]{1,0:T(8,128)(2,1)}, u32[]{:S(2)}, u32[]{:S(2)}) collective-permute-start(bf16[192,3584]{1,0:T(8,128)(2,1)} %get-tuple-element.24), channel_id=1, source_target_pairs={{0,2},{1,3},{2,4},{3,5},{4,6},{5,7},{6,0},{7,1},{8,10},{9,11},{10,... | collective-permute-start | bytes 4128776 | tf_op jit(solution)/shard_map/ppermute | solution.py:21
  114.0 33.3 %collective-permute-start.19 = (bf16[192,3584]{1,0:T(8,128)(2,1)}, bf16[192,3584]{1,0:T(8,128)(2,1)S(1)}, u32[]{:S(2)}, u32[]{:S(2)}) collective-permute-start(bf16[192,3584]{1,0:T(8,128)(2,1)} %get-tuple-element.25), channel_id=1, source_target_pairs={{0,6},{1,7},{2,0},{3,1},{4,2},{5,3},{6,4},{7,5},{8,14},{9,15},{10,... | collective-permute-start | bytes 4128776 | tf_op jit(solution)/shard_map/ppermute | solution.py:21
  114.6 93.0 %collective-permute-start.15 = (bf16[3584,512]{1,0:T(8,128)(2,1)}, bf16[3584,512]{1,0:T(8,128)(2,1)}, u32[]{:S(2)}, u32[]{:S(2)}) collective-permute-start(bf16[3584,512]{1,0:T(8,128)(2,1)} %bitcast.71), channel_id=1, source_target_pairs={{0,1},{1,0},{2,3},{3,2},{4,5},{5,4},{6,7},{7,6},{8,9},{9,8},{10,11... | collective-permute-start | bytes 11010056 | tf_op jit(solution)/shard_map/ppermute | solution.py:51
  114.6 97.5 %collective-permute-start.16 = (bf16[3584,512]{1,0:T(8,128)(2,1)}, bf16[3584,512]{1,0:T(8,128)(2,1)}, u32[]{:S(2)}, u32[]{:S(2)}) collective-permute-start(bf16[3584,512]{1,0:T(8,128)(2,1)} %bitcast.72), channel_id=1, source_target_pairs={{0,1},{1,0},{2,3},{3,2},{4,5},{5,4},{6,7},{7,6},{8,9},{9,8},{10,11... | collective-permute-start | bytes 11010056 | tf_op jit(solution)/shard_map/ppermute | solution.py:51
  115.1 55.3 %collective-permute-start.14 = (bf16[192,3584]{1,0:T(8,128)(2,1)}, bf16[192,3584]{1,0:T(8,128)(2,1)}, u32[]{:S(2)}, u32[]{:S(2)}) collective-permute-start(bf16[192,3584]{1,0:T(8,128)(2,1)} %get-tuple-element.23), channel_id=1, source_target_pairs={{0,4},{1,5},{2,6},{3,7},{4,0},{5,1},{6,2},{7,3},{8,12},{9,13},{10,... | collective-permute-start | bytes 4128776 | tf_op jit(solution)/shard_map/ppermute | solution.py:21
  117.3 7.5 %copy-start.3 = (bf16[192,3584]{1,0:T(8,128)(2,1)S(1)}, bf16[192,3584]{1,0:T(8,128)(2,1)}, u32[]{:S(2)}) copy-start(bf16[192,3584]{1,0:T(8,128)(2,1)} %get-tuple-element.22) | copy-start | bytes 4128772
  117.3 68.1 %all-to-all-start.2 = ((bf16[16,224,512]{2,1,0:T(8,128)(2,1)}), bf16[16,224,512]{2,1,0:T(8,128)(2,1)}, u32[]{:S(2)}, u32[]{:S(2)}) async-start(bf16[16,224,512]{2,1,0:T(8,128)(2,1)} %bitcast.73), calls=%async_computation.2 | async-start | bytes 7340032 | tf_op jit(solution)/shard_map/all_to_all | solution.py:60
  145.9 66.2 %collective-permute-start.17 = (bf16[512,3584]{1,0:T(8,128)(2,1)}, bf16[512,3584]{1,0:T(8,128)(2,1)}, u32[]{:S(2)}, u32[]{:S(2)}) collective-permute-start(bf16[512,3584]{1,0:T(8,128)(2,1)} %bitcast.74), channel_id=1, source_target_pairs={{0,1},{1,0},{2,3},{3,2},{4,5},{5,4},{6,7},{7,6},{8,9},{9,8},{10,11... | collective-permute-start | bytes 11010056 | tf_op jit(solution)/shard_map/ppermute | solution.py:51
  147.3 24.5 %copy-start.2 = (bf16[1,3584,512]{2,1,0:T(8,128)(2,1)S(1)}, bf16[1,3584,512]{2,1,0:T(8,128)(2,1)}, u32[]{:S(2)}) copy-start(bf16[1,3584,512]{2,1,0:T(8,128)(2,1)} %param.13) | copy-start | bytes 11010052
  147.5 25.9 %copy-start.12 = (bf16[384,3584]{1,0:T(8,128)(2,1)}, bf16[384,3584]{1,0:T(8,128)(2,1)S(1)}, u32[]{:S(2)}) copy-start(bf16[384,3584]{1,0:T(8,128)(2,1)S(1)} %constant_dynamic-update-slice_fusion.14) | copy-start | bytes 8257540
  171.8 1.6 copy-start.9
  185.4 8.4 %copy-start.10 = (bf16[384,3584]{1,0:T(8,128)(2,1)S(1)}, bf16[384,3584]{1,0:T(8,128)(2,1)}, u32[]{:S(2)}) copy-start(bf16[384,3584]{1,0:T(8,128)(2,1)} %copy-done.9) | copy-start | bytes 8257540
  185.4 49.4 %all-to-all-start.4 = ((bf16[16,32,3584]{2,1,0:T(8,128)(2,1)}), bf16[16,32,3584]{2,1,0:T(8,128)(2,1)}, u32[]{:S(2)}, u32[]{:S(2)}) async-start(bf16[16,32,3584]{2,1,0:T(8,128)(2,1)} %bitcast.75), calls=%async_computation.4 | async-start | bytes 7340032 | tf_op jit(solution)/shard_map/all_to_all | solution.py:60
  202.7 4.8 %copy-start.13 = (bf16[384,3584]{1,0:T(8,128)(2,1)S(1)}, bf16[384,3584]{1,0:T(8,128)(2,1)}, u32[]{:S(2)}) copy-start(bf16[384,3584]{1,0:T(8,128)(2,1)} %copy-done.12) | copy-start | bytes 8257540
  220.9 3.8 copy-start.11
  222.6 73.5 %collective-permute-start.20 = (bf16[192,3584]{1,0:T(8,128)(2,1)}, bf16[192,3584]{1,0:T(8,128)(2,1)}, u32[]{:S(2)}, u32[]{:S(2)}) collective-permute-start(bf16[192,3584]{1,0:T(8,128)(2,1)} %get-tuple-element.37), channel_id=1, source_target_pairs={{0,6},{1,7},{2,0},{3,1},{4,2},{5,3},{6,4},{7,5},{8,14},{9,15},{10,... | collective-permute-start | bytes 4128776 | tf_op jit(solution)/shard_map/ppermute | solution.py:21
  223.5 72.6 %collective-permute-start.22 = (bf16[192,3584]{1,0:T(8,128)(2,1)}, bf16[192,3584]{1,0:T(8,128)(2,1)}, u32[]{:S(2)}, u32[]{:S(2)}) collective-permute-start(bf16[192,3584]{1,0:T(8,128)(2,1)} %get-tuple-element.36), channel_id=1, source_target_pairs={{0,2},{1,3},{2,4},{3,5},{4,6},{5,7},{6,0},{7,1},{8,10},{9,11},{10,... | collective-permute-start | bytes 4128776 | tf_op jit(solution)/shard_map/ppermute | solution.py:21
  234.8 52.6 %all-to-all-start.1 = ((bf16[16,224,512]{2,1,0:T(8,128)(2,1)}), bf16[16,224,512]{2,1,0:T(8,128)(2,1)}, u32[]{:S(2)}, u32[]{:S(2)}) async-start(bf16[16,224,512]{2,1,0:T(8,128)(2,1)} %gather_fusion.1), calls=%async_computation.1 | async-start | bytes 7340032 | tf_op jit(solution)/shard_map/all_to_all | solution.py:62
  253.8 42.3 %collective-permute-start.21 = (bf16[192,3584]{1,0:T(8,128)(2,1)}, bf16[192,3584]{1,0:T(8,128)(2,1)S(1)}, u32[]{:S(2)}, u32[]{:S(2)}) collective-permute-start(bf16[192,3584]{1,0:T(8,128)(2,1)} %get-tuple-element.38), channel_id=1, source_target_pairs={{0,4},{1,5},{2,6},{3,7},{4,0},{5,1},{6,2},{7,3},{8,12},{9,13},{10,... | collective-permute-start | bytes 4128776 | tf_op jit(solution)/shard_map/ppermute | solution.py:21
  287.4 112.1 %all-to-all-start.3 = ((bf16[16,224,512]{2,1,0:T(8,128)(2,1)}), bf16[16,224,512]{2,1,0:T(8,128)(2,1)}, u32[]{:S(2)}, u32[]{:S(2)}) async-start(bf16[16,224,512]{2,1,0:T(8,128)(2,1)} %gather_fusion.2), calls=%async_computation.3 | async-start | bytes 7340032 | tf_op jit(solution)/shard_map/all_to_all | solution.py:62
  296.1 1.1 copy-start.18
  309.9 66.1 %collective-permute-start.26 = (bf16[128,3584]{1,0:T(8,128)(2,1)}, bf16[128,3584]{1,0:T(8,128)(2,1)S(1)}, u32[]{:S(2)}, u32[]{:S(2)}) collective-permute-start(bf16[128,3584]{1,0:T(8,128)(2,1)} %get-tuple-element.31), channel_id=1, source_target_pairs={{0,96},{8,104},{16,112},{24,120},{32,0},{40,8},{48,16},{56,24},{64... | collective-permute-start | bytes 2752520 | tf_op jit(solution)/shard_map/ppermute | solution.py:30
  310.8 65.2 %collective-permute-start.27 = (bf16[128,3584]{1,0:T(8,128)(2,1)}, bf16[128,3584]{1,0:T(8,128)(2,1)S(1)}, u32[]{:S(2)}, u32[]{:S(2)}) collective-permute-start(bf16[128,3584]{1,0:T(8,128)(2,1)} %get-tuple-element.32), channel_id=1, source_target_pairs={{0,32},{8,40},{16,48},{24,56},{32,64},{40,72},{48,80},{56,88},{64,... | collective-permute-start | bytes 2752520 | tf_op jit(solution)/shard_map/ppermute | solution.py:30
  313.2 63.8 %copy-start.7 = (bf16[128,3584]{1,0:T(8,128)(2,1)S(1)}, bf16[128,3584]{1,0:T(8,128)(2,1)}, u32[]{:S(2)}) copy-start(bf16[128,3584]{1,0:T(8,128)(2,1)} %get-tuple-element.30) | copy-start | bytes 2752516
  313.2 62.8 %collective-permute-start.28 = (bf16[128,3584]{1,0:T(8,128)(2,1)}, bf16[128,3584]{1,0:T(8,128)(2,1)}, u32[]{:S(2)}, u32[]{:S(2)}) collective-permute-start(bf16[128,3584]{1,0:T(8,128)(2,1)} %get-tuple-element.33), channel_id=1, source_target_pairs={{0,64},{8,72},{16,80},{24,88},{32,96},{40,104},{48,112},{56,120},{... | collective-permute-start | bytes 2752520 | tf_op jit(solution)/shard_map/ppermute | solution.py:30
  318.1 81.0 %copy-start.6 = (bf16[128,3584]{1,0:T(8,128)(2,1)S(1)}, bf16[128,3584]{1,0:T(8,128)(2,1)}, u32[]{:S(2)}) copy-start(bf16[128,3584]{1,0:T(8,128)(2,1)} %get-tuple-element.26) | copy-start | bytes 2752516
  318.1 60.9 %collective-permute-start.23 = (bf16[128,3584]{1,0:T(8,128)(2,1)}, bf16[128,3584]{1,0:T(8,128)(2,1)S(1)}, u32[]{:S(2)}, u32[]{:S(2)}) collective-permute-start(bf16[128,3584]{1,0:T(8,128)(2,1)} %get-tuple-element.27), channel_id=1, source_target_pairs={{0,24},{8,0},{16,8},{24,16},{32,56},{40,32},{48,40},{56,48},{64,88... | collective-permute-start | bytes 2752520 | tf_op jit(solution)/shard_map/ppermute | solution.py:30
  318.7 60.3 %collective-permute-start.24 = (bf16[128,3584]{1,0:T(8,128)(2,1)}, bf16[128,3584]{1,0:T(8,128)(2,1)S(1)}, u32[]{:S(2)}, u32[]{:S(2)}) collective-permute-start(bf16[128,3584]{1,0:T(8,128)(2,1)} %get-tuple-element.28), channel_id=1, source_target_pairs={{0,8},{8,16},{16,24},{24,0},{32,40},{40,48},{48,56},{56,32},{64,72... | collective-permute-start | bytes 2752520 | tf_op jit(solution)/shard_map/ppermute | solution.py:30
  376.0 23.1 %collective-permute-start.25 = (bf16[128,3584]{1,0:T(8,128)(2,1)}, bf16[128,3584]{1,0:T(8,128)(2,1)S(1)}, u32[]{:S(2)}, u32[]{:S(2)}) collective-permute-start(bf16[128,3584]{1,0:T(8,128)(2,1)} %get-tuple-element.29), channel_id=1, source_target_pairs={{0,16},{8,24},{16,0},{24,8},{32,48},{40,56},{48,32},{56,40},{64,80... | collective-permute-start | bytes 2752520 | tf_op jit(solution)/shard_map/ppermute | solution.py:30
  376.0 1.0 copy-start.8
  399.5 70.1 %all-to-all-start.5 = ((bf16[16,32,3584]{2,1,0:T(8,128)(2,1)}), bf16[16,32,3584]{2,1,0:T(8,128)(2,1)}, u32[]{:S(2)}, u32[]{:S(2)}) async-start(bf16[16,32,3584]{2,1,0:T(8,128)(2,1)} %gather_fusion.3), calls=%async_computation.5 | async-start | bytes 7340032 | tf_op jit(solution)/shard_map/all_to_all | solution.py:62
  405.0 47.3 %collective-permute-start.29 = (bf16[32,3584]{1,0:T(8,128)(2,1)S(1)}, bf16[32,3584]{1,0:T(8,128)(2,1)S(1)}, u32[]{:S(2)}, u32[]{:S(2)}) collective-permute-start(bf16[32,3584]{1,0:T(8,128)(2,1)S(1)} %get-tuple-element.40), channel_id=1, source_target_pairs={{0,96},{8,104},{16,112},{24,120},{32,0},{40,8},{48,16},{56,24},{64... | collective-permute-start | bytes 688136 | tf_op jit(solution)/shard_map/ppermute | solution.py:30
  405.9 47.7 %collective-permute-start.30 = (bf16[32,3584]{1,0:T(8,128)(2,1)S(1)}, bf16[32,3584]{1,0:T(8,128)(2,1)S(1)}, u32[]{:S(2)}, u32[]{:S(2)}) collective-permute-start(bf16[32,3584]{1,0:T(8,128)(2,1)S(1)} %get-tuple-element.42), channel_id=1, source_target_pairs={{0,32},{8,40},{16,48},{24,56},{32,64},{40,72},{48,80},{56,88},{64,... | collective-permute-start | bytes 688136 | tf_op jit(solution)/shard_map/ppermute | solution.py:30
  408.3 46.5 %collective-permute-start.31 = (bf16[32,3584]{1,0:T(8,128)(2,1)S(1)}, bf16[32,3584]{1,0:T(8,128)(2,1)S(1)}, u32[]{:S(2)}, u32[]{:S(2)}) collective-permute-start(bf16[32,3584]{1,0:T(8,128)(2,1)S(1)} %get-tuple-element.41), channel_id=1, source_target_pairs={{0,64},{8,72},{16,80},{24,88},{32,96},{40,104},{48,112},{56,120},{... | collective-permute-start | bytes 688136 | tf_op jit(solution)/shard_map/ppermute | solution.py:30
  408.6 46.3 %collective-permute-start.32 = (bf16[32,3584]{1,0:T(8,128)(2,1)S(1)}, bf16[32,3584]{1,0:T(8,128)(2,1)S(1)}, u32[]{:S(2)}, u32[]{:S(2)}) collective-permute-start(bf16[32,3584]{1,0:T(8,128)(2,1)S(1)} %get-tuple-element.43), channel_id=1, source_target_pairs={{0,24},{8,0},{16,8},{24,16},{32,56},{40,32},{48,40},{56,48},{64,88... | collective-permute-start | bytes 688136 | tf_op jit(solution)/shard_map/ppermute | solution.py:30
  409.3 45.7 %collective-permute-start.33 = (bf16[32,3584]{1,0:T(8,128)(2,1)S(1)}, bf16[32,3584]{1,0:T(8,128)(2,1)S(1)}, u32[]{:S(2)}, u32[]{:S(2)}) collective-permute-start(bf16[32,3584]{1,0:T(8,128)(2,1)S(1)} %get-tuple-element.45), channel_id=1, source_target_pairs={{0,8},{8,16},{16,24},{24,0},{32,40},{40,48},{48,56},{56,32},{64,72... | collective-permute-start | bytes 688136 | tf_op jit(solution)/shard_map/ppermute | solution.py:30
  452.3 7.5 %collective-permute-start.34 = (bf16[32,3584]{1,0:T(8,128)(2,1)S(1)}, bf16[32,3584]{1,0:T(8,128)(2,1)S(1)}, u32[]{:S(2)}, u32[]{:S(2)}) collective-permute-start(bf16[32,3584]{1,0:T(8,128)(2,1)S(1)} %get-tuple-element.44), channel_id=1, source_target_pairs={{0,16},{8,24},{16,0},{24,8},{32,48},{40,56},{48,32},{56,40},{64,80... | collective-permute-start | bytes 688136 | tf_op jit(solution)/shard_map/ppermute | solution.py:30
  469.6 4.4 copy-start.1
